TPU v7x, 512 devices: a whole 4x8x8 slice. The times are simulated.
512 devices in a mesh: xy: 32 (over x, z), gz: 16 (over y, core).
Axes of the slice: x: 4, y: 8, z: 8, core: 2. Of those that a mesh axis runs over, the one named last changes fastest.
Arguments:
- raw_tiles: bfloat16 [32, 32, 512, 512], P('gz', 'xy'), may hold values from -6 to 6
- src_tile: int32 [32, 1024, 1], P('gz'), may hold values from 0 to 31; in each aligned block of 32 rows (0 to 31, 32 to 63, ..., all dimensions but the last counted through in order) at most 2 rows name the same one
- shift_y: int32 [32, 1024], P('gz'), may hold values from 0 to 479
- shift_x: int32 [32, 1024], P('gz'), may hold values from 0 to 479
- subpixel: int32 [32, 1024], P('gz'), may hold values from 0 to 15
- owner_map: int32 [32], replicated, may hold values from 0 to 31, each once
- weight_one: bfloat16 [8, 1, 3, 3, 3], replicated, may hold values from -1.25 to 1.25
- bias_one: float32 [8], replicated, may hold values from -3 to 3
- weight_two: bfloat16 [8, 8, 3, 3, 3], replicated, may hold values from -0.4375 to 0.4375
- bias_two: float32 [8], replicated, may hold values from -3 to 3
Outputs:
- features: bfloat16 [8, 32, 2048, 512], P(None, 'gz', 'xy')
Inputs may be any that keep to these rules, and one draw needn't show every extreme that they name: `src_tile`: within the 32 subtiles of one device's strip of one section (aligned blocks), no source tile is named more than 2 times; some source tile is named exactly 2 times in some block. `owner_map`: A permutation; slot p is stored on the device of index p // 1 along xy.
All inputs are finite; a program needn't handle non-finite values.
Results may differ from a plain program's by a relative error of at most 0.0054.
Values may be sent and summed in bfloat16 or wider, within the bound.
No kernel may reach another device: no remote copies, remote signals or barrier semaphores. Data moves between devices by JAX's collectives and lax.ppermute only.
A program may use at most 64 MiB of HBM per device.

v0:
```python
import jax
import jax.numpy as jnp
from jax import lax
from jax.sharding import PartitionSpec as P

SUB = 32
SGY = 2
SGX = 16


def with_halo(cells, sides, width):
    for axis, dim in sides:
        count = lax.axis_size(axis)
        ends = count - 1
        head = lax.slice_in_dim(cells, 0, width, axis=dim)
        tail = lax.slice_in_dim(cells, cells.shape[dim] - width, cells.shape[dim], axis=dim)
        cells = jnp.concatenate(
            [
                lax.ppermute(tail, axis, [(i, (i + 1) % count) for i in range(ends)]),
                cells,
                lax.ppermute(head, axis, [((i + 1) % count, i) for i in range(ends)]),
            ],
            axis=dim,
        )
    return cells


def shift_cols(plane, offset):
    if offset == 1:
        return plane
    zero_col = jnp.zeros_like(plane[..., :1])
    if offset == 0:
        return jnp.concatenate([zero_col, plane[..., :-1]], axis=-1)
    return jnp.concatenate([plane[..., 1:], zero_col], axis=-1)


def convolve(extended, weight):
    chans = extended.shape[0]
    out_depth = extended.shape[1] - 2
    out_rows = extended.shape[2] - 2
    width = extended.shape[3]
    out_chans = weight.shape[0]
    matrix = jnp.transpose(weight, (0, 2, 3, 4, 1)).reshape(out_chans, 27 * chans)
    starts = list(range(0, out_rows, 16))

    def one_plane(plane):
        slab = lax.dynamic_slice_in_dim(extended, plane, 3, axis=1)
        blocks = []
        for start in starts:
            count = min(16, out_rows - start)
            columns = []
            for depth in range(3):
                for row_off in range(3):
                    for col_off in range(3):
                        columns.append(
                            shift_cols(
                                slab[:, depth, start + row_off : start + row_off + count, :],
                                col_off,
                            )
                        )
            stacked = jnp.concatenate(columns, axis=0).reshape(27 * chans, count * width)
            product = jnp.dot(matrix, stacked, preferred_element_type=jnp.float32)
            blocks.append(product.reshape(out_chans, count, width))
        return jnp.concatenate(blocks, axis=1)

    planes = lax.map(one_plane, jnp.arange(out_depth, dtype=jnp.int32))
    return jnp.transpose(planes, (1, 0, 2, 3))


def on_device(
    raw_tiles,
    src_tile,
    shift_y,
    shift_x,
    subpixel,
    owner_map,
    weight_one,
    bias_one,
    weight_two,
    bias_two,
):
    parts = lax.axis_size("xy")
    myself = lax.axis_index("xy")
    sections = raw_tiles.shape[0]
    src_dev = raw_tiles.shape[1]
    nsub = src_tile.shape[1]
    subs_dev = nsub // parts
    capacity = 2 * subs_dev // (parts * src_dev)
    slots = src_dev * capacity
    side = SUB
    source = src_tile[:, :, 0]
    stored = jnp.take(owner_map, source)
    holder = (stored // src_dev).reshape(sections, parts, subs_dev)
    within = (stored % src_dev).reshape(sections, parts, subs_dev)
    blocked = source.reshape(sections, parts, subs_dev)
    order = jnp.arange(subs_dev, dtype=jnp.int32)
    earlier = order[None, :] < order[:, None]
    same_tile = blocked[:, :, :, None] == blocked[:, :, None, :]
    rank = jnp.sum(jnp.logical_and(same_tile, earlier), axis=-1)
    slot_id = within * capacity + rank
    wanted = jnp.arange(slots, dtype=jnp.int32)
    match = jnp.logical_and(
        holder[:, :, None, :] == myself, slot_id[:, :, None, :] == wanted[:, None]
    )
    present = jnp.any(match, axis=-1)

    def pick(values):
        spread = values.reshape(sections, parts, 1, subs_dev)
        return jnp.sum(jnp.where(match, spread, 0), axis=-1)

    tops = pick(shift_y)
    lefts = pick(shift_x)
    codes = pick(subpixel)
    tile_of = jnp.broadcast_to(wanted // capacity, tops.shape)
    section_of = jnp.broadcast_to(jnp.arange(sections, dtype=jnp.int32)[:, None, None], tops.shape)

    def window(z, k, y, x):
        return lax.dynamic_slice(raw_tiles, (z, k, y, x), (1, 1, side + 1, side + 1))[0, 0]

    patches = jax.vmap(window)(
        section_of.reshape(-1), tile_of.reshape(-1), tops.reshape(-1), lefts.reshape(-1)
    ).astype(jnp.float32)
    flat_codes = codes.reshape(-1)
    frac_y = ((flat_codes // 4).astype(jnp.float32) / 4.0)[:, None, None]
    frac_x = ((flat_codes % 4).astype(jnp.float32) / 4.0)[:, None, None]
    rendered = (
        (1.0 - frac_y) * (1.0 - frac_x) * patches[:, :-1, :-1]
        + (1.0 - frac_y) * frac_x * patches[:, :-1, 1:]
        + frac_y * (1.0 - frac_x) * patches[:, 1:, :-1]
        + frac_y * frac_x * patches[:, 1:, 1:]
    )
    rendered = rendered * present.reshape(-1)[:, None, None].astype(jnp.float32)
    outgoing = rendered.astype(jnp.bfloat16).reshape(sections, parts, slots, side * side)
    outgoing = jnp.transpose(outgoing, (1, 0, 2, 3))
    received = lax.all_to_all(outgoing, "xy", split_axis=0, concat_axis=0, tiled=True)
    pool = jnp.transpose(received, (1, 0, 2, 3)).reshape(sections, parts * slots, side * side)
    mine_holder = lax.dynamic_index_in_dim(holder, myself, 1, keepdims=False)
    mine_slot = lax.dynamic_index_in_dim(slot_id, myself, 1, keepdims=False)
    row_index = mine_holder * slots + mine_slot
    arrived = jnp.take_along_axis(pool, row_index[:, :, None], axis=1)
    image = arrived.reshape(sections, SGY, SGX, side, side)
    image = jnp.transpose(image, (0, 1, 3, 2, 4)).reshape(sections, SGY * side, SGX * side)
    extended = with_halo(image, (("xy", 1), ("gz", 0)), 1)
    hidden = jax.nn.relu(
        convolve(extended[None], weight_one) + bias_one[:, None, None, None]
    ).astype(jnp.bfloat16)
    widened = with_halo(hidden, (("xy", 2), ("gz", 1)), 1)
    result = convolve(widened, weight_two) + bias_two[:, None, None, None]
    return result.astype(jnp.bfloat16)


def solution(mesh):
    in_specs = (
        P("gz", "xy", None, None),
        P("gz", None, None),
        P("gz", None),
        P("gz", None),
        P("gz", None),
        P(),
        P(),
        P(),
        P(),
        P(),
    )
    out_specs = P(None, "gz", "xy", None)
    return jax.shard_map(
        on_device, mesh=mesh, in_specs=in_specs, out_specs=out_specs, check_vma=False
    )
```

profile of v0, /device:TPU:27, one launch (start us, length us, event | category | flops | bytes accessed | tf_op | source)
XLA Modules:
  0.0 722.2 jit_solution(9718374905132131154)
XLA Ops:
  1.6 12.6 %gather_fusion = s32[2048]{0:T(1024)S(1)} fusion(s32[32]{0:T(128)S(1)} %copy-done, s32[2048]{0:T(1024)S(1)} %broadcast_clamp_fusion), kind=kCustom, calls=%fused_computation | custom fusion | bytes 24576 | tf_op jit(solution)/shard_map/jit(_take)/gather | solution.py:92
  17.5 515.3 %while.26 = (s32[]{:T(128)}, bf16[2,1,512,512]{3,2,1,0:T(8,128)(2,1)}, s32[128,4]{0,1:T(4,128)S(1)}, bf16[128,1,1,33,33]{4,3,2,1,0:T(8,128)(2,1)}) while((s32[]{:T(128)}, bf16[2,1,512,512]{3,2,1,0:T(8,128)(2,1)}, s32[128,4]{0,1:T(4,128)S(1)}, bf16[128,1,1,33,33]{4,3,2,1,0:T(8,128)(2,1)}) %tuple.530), condition=%wide.while_cond.clone, body=%wide.while_body.sunk.clone | while | flops 2 | bytes 22641 | solution.py:118
  22.2 3.4 bitcast_dynamic-update-slice_fusion.3
  26.2 3.4 bitcast_dynamic-update-slice_fusion.3
  46.3 3.4 bitcast_dynamic-update-slice_fusion.3
  50.4 3.4 bitcast_dynamic-update-slice_fusion.3
  66.4 3.4 bitcast_dynamic-update-slice_fusion.3
  70.5 3.4 bitcast_dynamic-update-slice_fusion.3
  122.8 3.4 bitcast_dynamic-update-slice_fusion.3
  150.9 3.4 bitcast_dynamic-update-slice_fusion.3
  163.0 3.4 bitcast_dynamic-update-slice_fusion.3
  175.1 3.4 bitcast_dynamic-update-slice_fusion.3
  191.2 3.4 bitcast_dynamic-update-slice_fusion.3
  195.3 3.4 bitcast_dynamic-update-slice_fusion.3
  219.4 3.4 bitcast_dynamic-update-slice_fusion.3
  223.4 3.4 bitcast_dynamic-update-slice_fusion.3
  227.5 3.4 bitcast_dynamic-update-slice_fusion.3
  239.5 3.4 bitcast_dynamic-update-slice_fusion.3
  243.6 3.4 bitcast_dynamic-update-slice_fusion.3
  271.7 3.4 bitcast_dynamic-update-slice_fusion.3
  279.8 3.4 bitcast_dynamic-update-slice_fusion.3
  291.9 3.4 bitcast_dynamic-update-slice_fusion.3
  295.9 3.4 bitcast_dynamic-update-slice_fusion.3
  304.0 3.4 bitcast_dynamic-update-slice_fusion.3
  352.2 3.4 bitcast_dynamic-update-slice_fusion.3
  356.2 3.4 bitcast_dynamic-update-slice_fusion.3
  376.4 3.4 bitcast_dynamic-update-slice_fusion.3
  384.4 3.4 bitcast_dynamic-update-slice_fusion.3
  392.5 3.4 bitcast_dynamic-update-slice_fusion.3
  396.5 3.4 bitcast_dynamic-update-slice_fusion.3
  408.6 3.4 bitcast_dynamic-update-slice_fusion.3
  436.8 3.4 bitcast_dynamic-update-slice_fusion.3
  460.9 3.4 bitcast_dynamic-update-slice_fusion.3
  464.9 3.4 bitcast_dynamic-update-slice_fusion.3
  509.2 3.4 bitcast_dynamic-update-slice_fusion.3
  513.3 3.4 bitcast_dynamic-update-slice_fusion.3
  517.3 3.4 bitcast_dynamic-update-slice_fusion.3
  525.3 3.4 bitcast_dynamic-update-slice_fusion.3
  541.2 13.0 %all-to-all-start = ((bf16[32,2,2,1024]{3,2,1,0:T(2,128)(2,1)}), bf16[32,2,2,1024]{3,2,1,0:T(2,128)(2,1)S(1)}, u32[]{:S(2)}, u32[]{:S(2)}) async-start(bf16[32,2,2,1024]{3,2,1,0:T(2,128)(2,1)} %copy.37), calls=%async_computation | async-start | bytes 524288 | tf_op jit(solution)/shard_map/all_to_all | solution.py:135
  555.7 7.3 %all-to-all-done = bf16[32,2,2,1024]{3,2,1,0:T(2,128)(2,1)S(1)} async-done(((bf16[32,2,2,1024]{3,2,1,0:T(2,128)(2,1)}), bf16[32,2,2,1024]{3,2,1,0:T(2,128)(2,1)S(1)}, u32[]{:S(2)}, u32[]{:S(2)}) %all-to-all-start) | async-done | bytes 262176 | tf_op jit(solution)/shard_map/all_to_all | solution.py:135
  565.6 5.2 collective-permute-start
  575.2 7.8 %collective-permute-start.2 = (bf16[1,66,512]{2,1,0:T(8,128)(2,1)S(1)}, bf16[1,66,512]{2,1,0:T(8,128)(2,1)S(1)}, u32[]{:S(2)}, u32[]{:S(2)}) collective-permute-start(bf16[1,66,512]{2,1,0:T(8,128)(2,1)S(1)} %get-tuple-element.465), channel_id=1, source_target_pairs={{0,1},{1,2},{2,3},{3,4},{4,5},{5,6},{6,7},{7,8},{8,9},{9,10},{10,1... | collective-permute-start | bytes 202760 | tf_op jit(solution)/shard_map/ppermute | solution.py:19
  585.4 4.6 collective-permute-done.3
  590.0 36.9 %while.24 = (s32[]{:T(128)}, f32[2,8,64,512]{3,1,2,0:T(8,128)}, s32[2]{0:T(128)S(1)}, bf16[1,4,66,512]{3,2,1,0:T(8,128)(2,1)S(1)}, bf16[8,27]{1,0:T(8,128)(2,1)S(1)}) while((s32[]{:T(128)}, f32[2,8,64,512]{3,1,2,0:T(8,128)}, s32[2]{0:T(128)S(1)}, bf16[1,4,66,512]{3,2,1,0:T(8,128)(2,1)S(1)}, bf16[8,27]{1,0:T(8,128)(2,1)S(1)}) %tuple.533), condition=%wide.region_6.7_spmd.clone, body=%wide.region_5.6_spmd.sunk.clone | while | flops 14942226 | bytes 18476800 | solution.py:66
  631.1 5.7 collective-permute-start.5
  642.7 4.2 collective-permute-done.6
  647.7 4.9 collective-permute-done.7
  654.1 65.0 %while.25 = (s32[]{:T(128)}, f32[2,8,64,512]{3,2,0,1:T(8,128)}, s32[2]{0:T(128)S(1)}, bf16[8,4,66,512]{3,0,2,1:T(8,128)(2,1)S(1)}, bf16[8,216]{1,0:T(8,128)(2,1)S(1)}) while((s32[]{:T(128)}, f32[2,8,64,512]{3,2,0,1:T(8,128)}, s32[2]{0:T(128)S(1)}, bf16[8,4,66,512]{3,0,2,1:T(8,128)(2,1)S(1)}, bf16[8,216]{1,0:T(8,128)(2,1)S(1)}) %tuple.536), condition=%wide.region_8.9_spmd.clone, body=%wide.region_7.8_spmd.sunk.clone | while | flops 114032656 | bytes 123167040 | solution.py:66
  (1493 shorter events, 507.6 us)
Async XLA Ops:
  0.0 1.5 copy-start
  1.5 12.9 %copy-start.5 = (s32[2,1024]{1,0:T(2,128)S(1)}, s32[2,1024]{1,0:T(2,128)}, u32[]{:S(2)}) copy-start(s32[2,1024]{1,0:T(2,128)} %param.18) | copy-start | bytes 24580
  1.5 13.0 %copy-start.6 = (s32[2,1024]{1,0:T(2,128)S(1)}, s32[2,1024]{1,0:T(2,128)}, u32[]{:S(2)}) copy-start(s32[2,1024]{1,0:T(2,128)} %param.16) | copy-start | bytes 24580
  1.6 13.1 %copy-start.7 = (s32[2,1024]{1,0:T(2,128)S(1)}, s32[2,1024]{1,0:T(2,128)}, u32[]{:S(2)}) copy-start(s32[2,1024]{1,0:T(2,128)} %param.17) | copy-start | bytes 24580
  541.2 44.0 %copy-start.4 = (bf16[8,1,3,3,3]{0,4,3,2,1:T(4,128)(2,1)S(1)}, bf16[8,1,3,3,3]{0,4,3,2,1:T(4,128)(2,1)}, u32[]{:S(2)}) copy-start(bf16[8,1,3,3,3]{0,4,3,2,1:T(4,128)(2,1)} %param.20) | copy-start | bytes 1300
  541.2 21.8 %all-to-all-start = ((bf16[32,2,2,1024]{3,2,1,0:T(2,128)(2,1)}), bf16[32,2,2,1024]{3,2,1,0:T(2,128)(2,1)S(1)}, u32[]{:S(2)}, u32[]{:S(2)}) async-start(bf16[32,2,2,1024]{3,2,1,0:T(2,128)(2,1)} %copy.37), calls=%async_computation | async-start | bytes 524288 | tf_op jit(solution)/shard_map/all_to_all | solution.py:135
  565.6 7.4 %collective-permute-start = (bf16[2,1,512]{2,1,0:T(2,128)(2,1)S(1)}, bf16[2,1,512]{2,1,0:T(2,128)(2,1)S(1)}, u32[]{:S(2)}, u32[]{:S(2)}) collective-permute-start(bf16[2,1,512]{2,1,0:T(2,128)(2,1)S(1)} %get-tuple-element.467), channel_id=1, source_target_pairs={{0,16},{16,32},{32,48},{48,64},{64,80},{80,96},{96,112},{112,128},... | collective-permute-start | bytes 6152 | tf_op jit(solution)/shard_map/ppermute | solution.py:19
  570.8 4.4 collective-permute-start.1
  575.2 10.1 %collective-permute-start.2 = (bf16[1,66,512]{2,1,0:T(8,128)(2,1)S(1)}, bf16[1,66,512]{2,1,0:T(8,128)(2,1)S(1)}, u32[]{:S(2)}, u32[]{:S(2)}) collective-permute-start(bf16[1,66,512]{2,1,0:T(8,128)(2,1)S(1)} %get-tuple-element.465), channel_id=1, source_target_pairs={{0,1},{1,2},{2,3},{3,4},{4,5},{5,6},{6,7},{7,8},{8,9},{9,10},{10,1... | collective-permute-start | bytes 202760 | tf_op jit(solution)/shard_map/ppermute | solution.py:19
  583.1 6.9 collective-permute-start.3
  590.0 36.9 %copy-start.8 = (f32[8]{0:T(128)S(1)}, f32[8]{0:T(128)}, u32[]{:S(2)}) copy-start(f32[8]{0:T(128)} %param.21) | copy-start | bytes 100
  626.9 15.6 %copy-start.3 = (bf16[8,8,3,3,3]{1,0,4,3,2:T(8,128)(2,1)S(1)}, bf16[8,8,3,3,3]{1,0,4,3,2:T(8,128)(2,1)}, u32[]{:S(2)}) copy-start(bf16[8,8,3,3,3]{1,0,4,3,2:T(8,128)(2,1)} %param.22) | copy-start | bytes 10372
  628.9 8.0 %collective-permute-start.4 = (bf16[8,2,1,512]{3,0,2,1:T(8,128)(2,1)S(1)}, bf16[8,2,1,512]{3,0,2,1:T(8,128)(2,1)S(1)}, u32[]{:S(2)}, u32[]{:S(2)}) collective-permute-start(bf16[8,2,1,512]{3,0,2,1:T(8,128)(2,1)S(1)} %get-tuple-element.463), channel_id=1, source_target_pairs={{0,16},{16,32},{32,48},{48,64},{64,80},{80,96},{96,112},{112,128},... | collective-permute-start | bytes 49160 | tf_op jit(solution)/shard_map/ppermute | solution.py:19
  631.1 6.5 collective-permute-start.5
  637.9 9.0 %collective-permute-start.6 = (bf16[8,1,66,512]{3,0,2,1:T(8,128)(2,1)S(1)}, bf16[8,1,66,512]{3,0,2,1:T(8,128)(2,1)S(1)}, u32[]{:S(2)}, u32[]{:S(2)}) collective-permute-start(bf16[8,1,66,512]{3,0,2,1:T(8,128)(2,1)S(1)} %get-tuple-element.461), channel_id=1, source_target_pairs={{0,1},{1,2},{2,3},{3,4},{4,5},{5,6},{6,7},{7,8},{8,9},{9,10},{10,1... | collective-permute-start | bytes 1622024 | tf_op jit(solution)/shard_map/ppermute | solution.py:19
  640.6 12.0 %collective-permute-start.7 = (bf16[8,1,66,512]{3,0,2,1:T(8,128)(2,1)S(1)}, bf16[8,1,66,512]{3,0,2,1:T(8,128)(2,1)}, u32[]{:S(2)}, u32[]{:S(2)}) collective-permute-start(bf16[8,1,66,512]{3,0,2,1:T(8,128)(2,1)S(1)} %get-tuple-element.462), channel_id=1, source_target_pairs={{1,0},{2,1},{3,2},{4,3},{5,4},{6,5},{7,6},{8,7},{9,8},{10,9},{11,1... | collective-permute-start | bytes 1622024 | tf_op jit(solution)/shard_map/ppermute | solution.py:21
  646.9 0.8 copy-start.2
  654.1 65.0 %copy-start.9 = (f32[8]{0:T(128)S(1)}, f32[8]{0:T(128)}, u32[]{:S(2)}) copy-start(f32[8]{0:T(128)} %param.23) | copy-start | bytes 100
  719.1 2.9 copy-start.1
where the time goes:
time: 734 us; the launch traced here: 722 us
  local copies, waits for them, and re-layouts  603 us (82%)
  starting transfers between devices  43 us (6%)
  loops' own time  27.7 us (4%)
  waiting for transfers between devices  23.9 us (3%)
  other arithmetic  17.8 us (2%)
    gather x384, local copies, waits for them, and re-layouts  515 us
    while x858, local copies, waits for them, and re-layouts  35.3 us
    another operation x2, loops' own time, convolve(): planes = lax.map(one_plane, jnp.arange(out_depth, dtype=jnp.int32))  27.5 us
    ppermute x4, starting transfers between devices, with_halo(): lax.ppermute(tail, axis, [(i, (i + 1) % count) for i in range(ends)])  18 us
  transfers between devices with their start and end apart: 9, of which 6 were waited for; matrix products, arithmetic and copies ran while one was open for 0% of the time, Pallas kernels for 0%

commit v1 on v0

v1 whole, which is shorter than its diff:
```python
import jax
import jax.numpy as jnp
from jax import lax
from jax.experimental import pallas as pl
from jax.experimental.pallas import tpu as pltpu
from jax.sharding import PartitionSpec as P

SUB = 32
W = 512
HID_ROWS = 22
WIN_ROWS = 24
IMG_ROWS = 80
F32 = jnp.float32
BF16 = jnp.bfloat16


def iota(shape, dim):
    return lax.broadcasted_iota(jnp.int32, shape, dim)


def by_index(which, choices):
    result = choices[-1]
    for number in range(len(choices) - 2, -1, -1):
        result = jnp.where(which == number, choices[number], result)
    return result


def render_kernel(table, tiles, out, wide):
    parts = out.shape[0]
    sections = tiles.shape[0]
    for z in range(sections):
        for t in range(4):
            wide[z, t] = tiles[z, :, 128 * t : 128 * t + 128].astype(F32)
    lane = iota((8, 128), 1)
    group = lane // 32
    lane_tall = iota((SUB, 128), 1)

    def one(q, z, slot):
        code = table[(z * parts + q) * 2 + slot]
        y = code & 511
        x = (code >> 9) & 511
        a = ((code >> 20) & 3).astype(F32) * 0.25
        b = ((code >> 18) & 3).astype(F32) * 0.25
        near = x >> 7
        far = jnp.minimum(near + 1, 3)
        low = x & 127
        wraps = lane_tall < low
        upper = jnp.where(wraps, wide[z, far, pl.ds(y, SUB), :], wide[z, near, pl.ds(y, SUB), :])
        lower = jnp.where(
            wraps, wide[z, far, pl.ds(y + 1, SUB), :], wide[z, near, pl.ds(y + 1, SUB), :]
        )
        mixed = (1.0 - a) * upper + a * lower
        here, right = [], []
        for g in range(4):
            piece = mixed[8 * g : 8 * g + 8]
            here.append(pltpu.roll(piece, (32 * g + 128 - low) & 127, 1))
            right.append(pltpu.roll(piece, (32 * g + 127 - low) & 127, 1))
        value = (1.0 - b) * by_index(group, here) + b * by_index(group, right)
        out[q, z * 2 + slot] = value.astype(BF16)

    @pl.loop(0, parts)
    def _(q):
        for z in range(sections):
            for slot in range(2):
                one(q, z, slot)

    sub = iota((8, 128), 0)
    which = jnp.where(sub < 4, group, (group + 1) & 3)

    @pl.loop(0, parts)
    def _(q):
        after = jnp.minimum(q + 1, parts - 1)
        before = jnp.maximum(q - 1, 0)
        turned = []
        for zs in range(4):
            both = jnp.where(sub < 4, out[after, zs].astype(F32), out[before, zs].astype(F32))
            turned.append(both if zs == 0 else pltpu.roll(both, 32 * zs, 1))
        out[q, 4] = by_index(which, turned).astype(BF16)


def assemble_kernel(table, flags, pool, image):
    lane = iota((8, 128), 1)
    group = lane // 32
    sections = image.shape[0]

    def entry(z, strip, s):
        packed = table[(z * 3 + strip) * 32 + s]
        return packed >> 1, 2 * z + (packed & 1)

    for z in range(sections):
        for c in range(4):
            rows = []
            heads, feet = [], []
            for v in range(4):
                k, zs = entry(z, 0, 16 + 4 * c + v)
                piece = pool[k, 4].astype(F32)
                heads.append(pltpu.roll(piece, (32 * (v - zs - 3) + 256) & 127, 1))
                k, zs = entry(z, 2, 4 * c + v)
                piece = pool[k, 4].astype(F32)
                feet.append(pltpu.roll(piece, (32 * (v - zs) + 256) & 127, 1))
            rows.append(jnp.where(flags[0] == 0, 0.0, by_index(group, heads)))
            for u in range(2):
                blocks = []
                for v in range(4):
                    k, zs = entry(z, 1, 16 * u + 4 * c + v)
                    blocks.append(pool[k, zs].astype(F32))
                for g in range(4):
                    turned = [
                        blocks[v] if v == g else pltpu.roll(blocks[v], (32 * (v - g)) % 128, 1)
                        for v in range(4)
                    ]
                    rows.append(by_index(group, turned))
            rows.append(jnp.where(flags[1] == 0, 0.0, by_index(group, feet)))
            image[z, :, 128 * c : 128 * c + 128] = jnp.concatenate(rows, axis=0).astype(BF16)


def band_kernel(flat_one, flat_two, one, two):
    rows, cols = one.shape
    col = iota((27, cols), 1)
    base = (col // WIN_ROWS) % 3 * 9 + col // (3 * WIN_ROWS)
    offset = iota((rows, cols), 1) % WIN_ROWS - iota((rows, cols), 0) // 8
    total = jnp.zeros((rows, cols), F32)
    for e in range(3):
        picks = (iota((27, cols), 0) == base + 3 * e).astype(F32).astype(BF16)
        taps = jnp.dot(flat_one[...], picks, preferred_element_type=F32)
        total = jnp.where(offset == e, jnp.concatenate([taps] * (rows // 8), axis=0), total)
    one[...] = total.astype(BF16)

    rows, cols = two.shape
    col = iota((216, cols), 1)
    base = col % 8 * 27 + col // 80 * 9
    spread = (iota((rows, 24), 0) // 8 == iota((rows, 24), 1)).astype(F32).astype(BF16)
    offset = iota((rows, cols), 1) % 80 // 8 - iota((rows, cols), 0) % 8
    total = jnp.zeros((rows, cols), F32)
    for e in range(3):
        parts = []
        for f in range(3):
            picks = (iota((216, cols), 0) == base + (3 * e + f)).astype(F32).astype(BF16)
            parts.append(jnp.dot(flat_two[...], picks, preferred_element_type=F32))
        taps = jnp.concatenate(parts, axis=0).astype(BF16)
        total = jnp.where(offset == e, jnp.dot(spread, taps, preferred_element_type=F32), total)
    two[...] = total.astype(BF16)


def conv_kernel(flags, bias_two, bias_one, before, own, after, one, two, out, shifted, hidden):
    lane = iota((IMG_ROWS, W), 1)
    for number, (ref, z) in enumerate(
        [(before, 0), (before, 1), (own, 0), (own, 1), (after, 0), (after, 1)]
    ):
        plane = ref[z].astype(F32)
        shifted[number, 0] = jnp.where(lane == 0, 0.0, pltpu.roll(plane, 1, 1))
        shifted[number, 1] = plane
        shifted[number, 2] = jnp.where(lane == W - 1, 0.0, pltpu.roll(plane, W - 1, 1))
    gain = bias_one[...][:, :1]
    height = HID_ROWS * 8
    row = iota((height, W), 0)
    for p in range(4):
        for b in range(3):
            start = HID_ROWS * b + 6
            stack = jnp.concatenate(
                [
                    shifted[p + d, f, start : start + WIN_ROWS, :]
                    for f in range(3)
                    for d in range(3)
                ],
                axis=0,
            ).astype(BF16)
            total = jnp.dot(one[...], stack, preferred_element_type=F32)
            total = jnp.maximum(total.reshape(HID_ROWS, 8, W) + gain, 0.0).reshape(height, W)
            if b == 0:
                total = jnp.where(jnp.logical_or(row >= 8, flags[0] != 0), total, 0.0)
            if b == 2:
                total = jnp.where(jnp.logical_or(row < height - 8, flags[1] != 0), total, 0.0)
            hidden[p, height * b : height * b + height, :] = total.astype(BF16)

    @pl.when(flags[2] == 0)
    def _():
        hidden[0] = jnp.zeros(hidden.shape[1:], BF16)

    @pl.when(flags[3] == 0)
    def _():
        hidden[3] = jnp.zeros(hidden.shape[1:], BF16)

    edge = iota((64, W), 1)
    for z in range(2):
        for pair in range(4):
            halves = []
            for b in (2 * pair, 2 * pair + 1):
                stack = jnp.concatenate(
                    [hidden[z + d, 64 * b : 64 * b + 80, :] for d in range(3)], axis=0
                )
                total = jnp.dot(two[...], stack, preferred_element_type=F32)
                left = jnp.where(edge == 0, 0.0, pltpu.roll(total[0:64], 1, 1))
                right = jnp.where(edge == W - 1, 0.0, pltpu.roll(total[128:192], W - 1, 1))
                halves.append(total[64:128] + left + right)
            for o in range(8):
                both = jnp.concatenate([half[8 * o : 8 * o + 8] for half in halves], axis=0)
                out[o, z, 16 * pair : 16 * pair + 16, :] = (both + bias_two[o]).astype(BF16)


def smem():
    return pl.BlockSpec(memory_space=pltpu.SMEM)


def vmem():
    return pl.BlockSpec(memory_space=pltpu.VMEM)


def on_device(
    raw_tiles,
    src_tile,
    shift_y,
    shift_x,
    subpixel,
    owner_map,
    weight_one,
    bias_one,
    weight_two,
    bias_two,
):
    parts = lax.axis_size("xy")
    depth = lax.axis_size("gz")
    me = lax.axis_index("xy")
    deep = lax.axis_index("gz")
    sections = raw_tiles.shape[0]
    source = src_tile.reshape(sections, parts, 32)
    packed = (shift_y + (shift_x << 9) + (subpixel << 18)).reshape(sections, parts, 32)
    tile_ids = jnp.arange(parts, dtype=jnp.int32)
    mine = jnp.sum(jnp.where(owner_map == me, tile_ids, 0))
    number = jnp.arange(32, dtype=jnp.int32)
    match = source == mine
    first = jnp.min(jnp.where(match, number, 31), axis=-1)
    last = jnp.max(jnp.where(match, number, 0), axis=-1)
    chosen = jnp.stack([first, last], axis=-1)
    table = jnp.sum(
        jnp.where(chosen[..., None] == number, packed[:, :, None, :], 0), axis=-1
    ).reshape(-1)

    outgoing = pl.pallas_call(
        render_kernel,
        out_shape=jax.ShapeDtypeStruct((parts, 5, 8, 128), BF16),
        in_specs=[smem(), vmem()],
        out_specs=vmem(),
        scratch_shapes=[pltpu.VMEM((sections, 4, 512, 128), F32)],
        name="render",
    )(table, raw_tiles.reshape(sections, 512, 512))

    received = lax.all_to_all(outgoing, "xy", split_axis=0, concat_axis=0, tiled=True)

    around = jnp.clip(me + jnp.arange(-1, 2, dtype=jnp.int32), 0, parts - 1)
    near = jnp.sum(
        jnp.where(
            around[None, :, None, None] == tile_ids[None, None, :, None], source[:, None], 0
        ),
        axis=2,
    )
    holder = jnp.sum(jnp.where(near[..., None] == tile_ids, owner_map, 0), axis=-1)
    second = jnp.any(
        jnp.logical_and(
            near[..., :, None] == near[..., None, :], number[None, :] < number[:, None]
        ),
        axis=-1,
    )
    places = (holder * 2 + second.astype(jnp.int32)).reshape(-1)
    flags = jnp.stack([me > 0, me < parts - 1, deep > 0, deep < depth - 1]).astype(jnp.int32)

    image = pl.pallas_call(
        assemble_kernel,
        out_shape=jax.ShapeDtypeStruct((sections, IMG_ROWS, W), BF16),
        in_specs=[smem(), smem(), vmem()],
        out_specs=vmem(),
        name="assemble",
    )(places, flags, received)

    before = lax.ppermute(image, "gz", [(i, i + 1) for i in range(depth - 1)])
    after = lax.ppermute(image, "gz", [(i + 1, i) for i in range(depth - 1)])

    banded_one, banded_two = pl.pallas_call(
        band_kernel,
        out_shape=(
            jax.ShapeDtypeStruct((HID_ROWS * 8, 9 * WIN_ROWS), BF16),
            jax.ShapeDtypeStruct((192, 240), BF16),
        ),
        in_specs=[vmem(), vmem()],
        out_specs=(vmem(), vmem()),
        name="bands",
    )(weight_one.reshape(8, 27), weight_two.reshape(8, 216))

    return pl.pallas_call(
        conv_kernel,
        out_shape=jax.ShapeDtypeStruct((8, sections, 64, W), BF16),
        in_specs=[smem(), smem()] + [vmem()] * 6,
        out_specs=vmem(),
        scratch_shapes=[
            pltpu.VMEM((6, 3, IMG_ROWS, W), F32),
            pltpu.VMEM((4, 66 * 8, W), BF16),
        ],
        name="convolve",
    )(
        flags,
        bias_two,
        jnp.broadcast_to(bias_one[:, None], (8, 128)),
        before,
        image,
        after,
        banded_one,
        banded_two,
    )


def solution(mesh):
    in_specs = (
        P("gz", "xy", None, None),
        P("gz", None, None),
        P("gz", None),
        P("gz", None),
        P("gz", None),
        P(),
        P(),
        P(),
        P(),
        P(),
    )
    out_specs = P(None, "gz", "xy", None)
    return jax.shard_map(
        on_device, mesh=mesh, in_specs=in_specs, out_specs=out_specs, check_vma=False
    )
```

time: 734 us -> 59.2 us (0.08)
  the two profiles are of different devices: /device:TPU:27 before, /device:TPU:25 now
where the time goes in v1:
time: 59.2 us; the launch traced here: 58.8 us
  starting transfers between devices  23.4 us (40%)
  Pallas kernels  17.4 us (29%)
  waiting for transfers between devices  8.16 us (14%)
  local copies, waits for them, and re-layouts  5.8 us (10%)
  other arithmetic  3.74 us (6%)
    all_to_all x1, starting transfers between devices, on_device(): lax.all_to_all(outgoing, 'xy', split_axis=0, concat_axis=0, tiled=True)  12.9 us
    pallas_call x1, Pallas kernels, on_device(): pl.pallas_call(render_kernel, out_shape=jax.ShapeDtypeStruct((parts, 5, 8...  8.35 us
    all_to_all x1, waiting for transfers between devices, on_device(): lax.all_to_all(outgoing, 'xy', split_axis=0, concat_axis=0, tiled=True)  8.16 us
    ppermute x1, starting transfers between devices, on_device(): after = lax.ppermute(image, 'gz', [(i + 1, i) for i in range(depth - 1)])  6.24 us
    pallas_call x1, Pallas kernels, on_device(): pl.pallas_call(conv_kernel, out_shape=jax.ShapeDtypeStruct((8, sections,...  4.99 us
    ppermute x1, starting transfers between devices, on_device(): before = lax.ppermute(image, 'gz', [(i, i + 1) for i in range(depth - 1)])  4.31 us
    pallas_call x1, Pallas kernels, on_device(): pl.pallas_call(band_kernel, out_shape=(jax.ShapeDtypeStruct((HID_ROWS * 8...  2.11 us
    unnamed x21, local copies, waits for them, and re-layouts  2.09 us
  transfers between devices with their start and end apart: 3, of which 1 were waited for; matrix products, arithmetic and copies ran while one was open for 6% of the time, Pallas kernels for 4%

profile of v1, /device:TPU:25, one launch (start us, length us, event | category | flops | bytes accessed | tf_op | source)
XLA Modules:
  0.0 58.8 jit_solution(17956676111842401874)
XLA Ops:
  0.0 0.7 %reduce = s32[2,1024]{1,0:T(2,128)S(1)} reduce(s32[2,1024,1]{1,2,0:T(1,128)} %param.11, s32[]{:T(128)} %constant.5.clone.1), dimensions={2}, to_apply=%param.11.reduce_sub_computation | reduce | bytes 16388 | tf_op args[1]
  0.7 0.0 copy-start.8
  0.7 0.1 broadcast_in_dim.79
  0.8 0.6 copy-done.8
  1.4 0.6 %fusion = s32[]{:T(128)} fusion(s32[32]{0:T(128)S(1)} %copy-done.8, s32[]{:T(128)S(6)} %axis_index.23), kind=kLoop, calls=%fused_computation.16 | loop fusion | flops 95 | bytes 136 | tf_op jit(solution)/shard_map/reduce_sum | solution.py:229
  2.0 0.0 copy-start.6
  2.0 0.0 copy-start.7
  2.0 0.8 %select_reduce_fusion.4 = (s32[2,32]{1,0:T(2,128)S(1)}, s32[2,32]{1,0:T(2,128)S(1)}) fusion(s32[2,32,32]{2,1,0:T(8,128)S(1)} %broadcast_in_dim.79, s32[]{:T(128)} %fusion), kind=kLoop, calls=%fused_computation.7 | loop fusion | flops 10112 | bytes 8708 | tf_op jit(solution)/shard_map/reduce_min | solution.py:232
  2.8 0.0 copy-start.5
  2.9 0.0 copy-done.6
  2.9 0.0 copy-done.7
  2.9 0.6 %copy-done.5 = s32[2,1024]{1,0:T(2,128)S(1)} copy-done((s32[2,1024]{1,0:T(2,128)S(1)}, s32[2,1024]{1,0:T(2,128)}, u32[]{:S(2)}) %copy-start.5) | copy-done | bytes 8216
  3.6 0.1 broadcast_in_dim.88
  3.6 0.2 select_reduce_fusion.2
  3.9 0.1 copy.19
  4.0 0.7 %reshape.78.table = s32[128]{0:T(128)} reshape(s32[2,32,2]{2,1,0:T(8,128)S(1)} %copy.19) | data formatting | bytes 1024 | tf_op jit(solution)/shard_map/reshape | solution.py:237
  4.7 8.3 %render.1 = bf16[32,5,8,128]{3,2,1,0:T(8,128)(2,1)} custom-call(s32[128]{0:T(128)} %reshape.78.table, bf16[2,512,512]{2,1,0:T(8,128)(2,1)} %bitcast.11), custom_call_target="tpu_custom_call" | custom-call | tf_op jit(solution)/shard_map/render/pallas_call | solution.py:239
  13.1 12.9 %all-to-all-start = ((bf16[32,5,8,128]{3,2,1,0:T(8,128)(2,1)}), bf16[32,5,8,128]{3,2,1,0:T(8,128)(2,1)S(1)}, u32[]{:S(2)}, u32[]{:S(2)}) async-start(bf16[32,5,8,128]{3,2,1,0:T(8,128)(2,1)} %render.1), calls=%async_computation | async-start | bytes 655360 | tf_op jit(solution)/shard_map/all_to_all | solution.py:248
  26.0 0.1 iota_compare_fusion.3
  26.1 0.1 select_reduce_fusion.1
  26.2 0.3 select_reduce_fusion
  26.4 0.3 and_reduce_fusion
  26.7 0.6 %add.34.table = s32[192]{0:T(256)} reshape(s32[2,3,32]{2,1,0:T(4,128)S(1)} %convert_add_fusion) | data formatting | bytes 1536 | tf_op jit(solution)/shard_map/add | solution.py:264
  27.4 0.6 %add_convert_fusion.flags = s32[4]{0:T(128)} fusion(pred[1]{0:T(512)(128)(4,1)} %bitcast.3, pred[1]{0:T(512)(128)(4,1)} %bitcast.2, pred[1]{0:T(512)(128)(4,1)} %bitcast.1, pred[1]{0:T(512)(128)(4,1)} %bitcast), kind=kLoop, calls=%fused_computation.14 | loop fusion | flops 16 | bytes 20 | tf_op jit(solution)/shard_map/convert_element_type | solution.py:265
  28.0 0.0 copy-start.4
  28.0 8.2 %all-to-all-done.pool = bf16[32,5,8,128]{3,2,1,0:T(8,128)(2,1)S(1)} async-done(((bf16[32,5,8,128]{3,2,1,0:T(8,128)(2,1)}), bf16[32,5,8,128]{3,2,1,0:T(8,128)(2,1)S(1)}, u32[]{:S(2)}, u32[]{:S(2)}) %all-to-all-start) | async-done | bytes 327712 | tf_op jit(solution)/shard_map/all_to_all | solution.py:248
  36.1 0.0 copy-start
  36.1 0.7 %copy-done = bf16[32,5,8,128]{3,2,1,0:T(8,128)(2,1)} copy-done((bf16[32,5,8,128]{3,2,1,0:T(8,128)(2,1)}, bf16[32,5,8,128]{3,2,1,0:T(8,128)(2,1)S(1)}, u32[]{:S(2)}) %copy-start) | copy-done | bytes 327704
  36.9 0.0 copy-start.3
  36.9 2.0 %assemble.1.own = bf16[2,80,512]{2,1,0:T(8,128)(2,1)} custom-call(s32[192]{0:T(256)} %add.34.table, s32[4]{0:T(128)} %add_convert_fusion.flags, bf16[32,5,8,128]{3,2,1,0:T(8,128)(2,1)} %copy-done), custom_call_target="tpu_custom_call" | custom-call | tf_op jit(solution)/shard_map/assemble/pallas_call | solution.py:267
  38.9 6.2 %collective-permute-start.1 = (bf16[2,80,512]{2,1,0:T(8,128)(2,1)}, bf16[2,80,512]{2,1,0:T(8,128)(2,1)S(1)}, u32[]{:S(2)}, u32[]{:S(2)}) collective-permute-start(bf16[2,80,512]{2,1,0:T(8,128)(2,1)} %assemble.1.own), channel_id=1, source_target_pairs={{1,0},{2,1},{3,2},{4,3},{5,4},{6,5},{7,6},{8,7},{9,8},{10,9},{11,1... | collective-permute-start | bytes 491528 | tf_op jit(solution)/shard_map/ppermute | solution.py:276
  45.1 4.3 %collective-permute-start = (bf16[2,80,512]{2,1,0:T(8,128)(2,1)}, bf16[2,80,512]{2,1,0:T(8,128)(2,1)S(1)}, u32[]{:S(2)}, u32[]{:S(2)}) collective-permute-start(bf16[2,80,512]{2,1,0:T(8,128)(2,1)} %assemble.1.own), channel_id=1, source_target_pairs={{0,1},{1,2},{2,3},{3,4},{4,5},{5,6},{6,7},{7,8},{8,9},{9,10},{10,1... | collective-permute-start | bytes 491528 | tf_op jit(solution)/shard_map/ppermute | solution.py:275
  49.4 0.0 copy-done.4
  49.4 0.6 %copy.21.flat_one = bf16[8,27]{1,0:T(8,128)(2,1)} copy(bf16[8,27]{0,1:T(8,128)(2,1)S(1)} %reshape.80) | data formatting | bytes 864 | tf_op jit(solution)/shard_map/reshape | solution.py:287
  50.1 0.0 copy-done.3
  50.1 0.1 copy.20
  50.3 0.7 %copy.22.flat_two = bf16[8,216]{1,0:T(8,128)(2,1)} copy(bf16[8,216]{0,1:T(8,128)(2,1)S(1)} %reshape.81) | data formatting | bytes 6912 | tf_op jit(solution)/shard_map/reshape | solution.py:287
  50.9 0.0 copy-start.9
  50.9 2.1 %bands.1 = (bf16[176,216]{1,0:T(8,128)(2,1)}, bf16[192,240]{1,0:T(8,128)(2,1)}) custom-call(bf16[8,27]{1,0:T(8,128)(2,1)} %copy.21.flat_one, bf16[8,216]{1,0:T(8,128)(2,1)} %copy.22.flat_two), custom_call_target="tpu_custom_call" | custom-call | tf_op jit(solution)/shard_map/bands/pallas_call | solution.py:278
  53.0 0.0 collective-permute-done.1.after
  53.0 0.0 copy-start.1
  53.1 0.0 collective-permute-done.before
  53.1 0.0 copy-done.9
  53.1 0.0 copy-start.2
  53.1 0.7 %broadcast_in_dim.77.bias_one = f32[8,128]{1,0:T(8,128)} broadcast(f32[8]{0:T(128)S(1)} %copy-done.9), dimensions={0} | broadcast | bytes 4128 | tf_op jit(solution)/shard_map/broadcast_in_dim | solution.py:302
  53.7 0.0 copy-done.1
  53.7 0.0 copy-done.2
  53.8 5.0 %convolve.1 = bf16[8,2,64,512]{3,2,1,0:T(8,128)(2,1)} custom-call(s32[4]{0:T(128)} %add_convert_fusion.flags, f32[8]{0:T(128)} %bias_two.1, f32[8,128]{1,0:T(8,128)} %broadcast_in_dim.77.bias_one, bf16[2,80,512]{2,1,0:T(8,128)(2,1)} %copy-done.2, bf16[2,80,512]{2,1,0:T(8,128)(2,1)} %assemble.1.own, bf16[2,80,512]{2,1,0:T(8,128)(2,1)} %copy-done.1, ...), custom_call_target="tpu_custom_call" | custom-call | tf_op jit(solution)/shard_map/convolve/pallas_call | solution.py:289
  (8 shorter events, 0.1 us)
Async XLA Ops:
  0.7 0.7 %copy-start.8 = (s32[32]{0:T(128)S(1)}, s32[32]{0:T(128)}, u32[]{:S(2)}) copy-start(s32[32]{0:T(128)} %param.15) | copy-start | bytes 388
  2.0 0.9 %copy-start.6 = (s32[2,1024]{1,0:T(2,128)S(1)}, s32[2,1024]{1,0:T(2,128)}, u32[]{:S(2)}) copy-start(s32[2,1024]{1,0:T(2,128)} %param.12) | copy-start | bytes 24580
  2.0 0.9 %copy-start.7 = (s32[2,1024]{1,0:T(2,128)S(1)}, s32[2,1024]{1,0:T(2,128)}, u32[]{:S(2)}) copy-start(s32[2,1024]{1,0:T(2,128)} %param.13) | copy-start | bytes 24580
  2.8 0.7 %copy-start.5 = (s32[2,1024]{1,0:T(2,128)S(1)}, s32[2,1024]{1,0:T(2,128)}, u32[]{:S(2)}) copy-start(s32[2,1024]{1,0:T(2,128)} %param.14) | copy-start | bytes 24580
  13.1 23.1 %all-to-all-start = ((bf16[32,5,8,128]{3,2,1,0:T(8,128)(2,1)}), bf16[32,5,8,128]{3,2,1,0:T(8,128)(2,1)S(1)}, u32[]{:S(2)}, u32[]{:S(2)}) async-start(bf16[32,5,8,128]{3,2,1,0:T(8,128)(2,1)} %render.1), calls=%async_computation | async-start | bytes 655360 | tf_op jit(solution)/shard_map/all_to_all | solution.py:248
  28.0 21.5 %copy-start.4 = (bf16[8,1,3,3,3]{0,4,3,2,1:T(4,128)(2,1)S(1)}, bf16[8,1,3,3,3]{0,4,3,2,1:T(4,128)(2,1)}, u32[]{:S(2)}) copy-start(bf16[8,1,3,3,3]{0,4,3,2,1:T(4,128)(2,1)} %param.16) | copy-start | bytes 1300
  36.1 0.7 %copy-start = (bf16[32,5,8,128]{3,2,1,0:T(8,128)(2,1)}, bf16[32,5,8,128]{3,2,1,0:T(8,128)(2,1)S(1)}, u32[]{:S(2)}) copy-start(bf16[32,5,8,128]{3,2,1,0:T(8,128)(2,1)S(1)} %all-to-all-done.pool) | copy-start | bytes 983044
  36.9 13.2 %copy-start.3 = (bf16[8,8,3,3,3]{1,0,4,3,2:T(8,128)(2,1)S(1)}, bf16[8,8,3,3,3]{1,0,4,3,2:T(8,128)(2,1)}, u32[]{:S(2)}) copy-start(bf16[8,8,3,3,3]{1,0,4,3,2:T(8,128)(2,1)} %param.18) | copy-start | bytes 10372
  38.9 14.2 %collective-permute-start.1 = (bf16[2,80,512]{2,1,0:T(8,128)(2,1)}, bf16[2,80,512]{2,1,0:T(8,128)(2,1)S(1)}, u32[]{:S(2)}, u32[]{:S(2)}) collective-permute-start(bf16[2,80,512]{2,1,0:T(8,128)(2,1)} %assemble.1.own), channel_id=1, source_target_pairs={{1,0},{2,1},{3,2},{4,3},{5,4},{6,5},{7,6},{8,7},{9,8},{10,9},{11,1... | collective-permute-start | bytes 491528 | tf_op jit(solution)/shard_map/ppermute | solution.py:276
  45.1 8.0 %collective-permute-start = (bf16[2,80,512]{2,1,0:T(8,128)(2,1)}, bf16[2,80,512]{2,1,0:T(8,128)(2,1)S(1)}, u32[]{:S(2)}, u32[]{:S(2)}) collective-permute-start(bf16[2,80,512]{2,1,0:T(8,128)(2,1)} %assemble.1.own), channel_id=1, source_target_pairs={{0,1},{1,2},{2,3},{3,4},{4,5},{5,6},{6,7},{7,8},{8,9},{9,10},{10,1... | collective-permute-start | bytes 491528 | tf_op jit(solution)/shard_map/ppermute | solution.py:275
  50.9 2.1 %copy-start.9 = (f32[8]{0:T(128)S(1)}, f32[8]{0:T(128)}, u32[]{:S(2)}) copy-start(f32[8]{0:T(128)} %param.17) | copy-start | bytes 100
  53.0 0.7 %copy-start.1 = (bf16[2,80,512]{2,1,0:T(8,128)(2,1)}, bf16[2,80,512]{2,1,0:T(8,128)(2,1)S(1)}, u32[]{:S(2)}) copy-start(bf16[2,80,512]{2,1,0:T(8,128)(2,1)S(1)} %collective-permute-done.1.after) | copy-start | bytes 491524
  53.1 0.7 %copy-start.2 = (bf16[2,80,512]{2,1,0:T(8,128)(2,1)}, bf16[2,80,512]{2,1,0:T(8,128)(2,1)S(1)}, u32[]{:S(2)}) copy-start(bf16[2,80,512]{2,1,0:T(8,128)(2,1)S(1)} %collective-permute-done.before) | copy-start | bytes 491524

commit v2 on v1

--- a/solution.py
+++ b/solution.py
@@ -10,6 +10,8 @@
 HID_ROWS = 22
 WIN_ROWS = 24
 IMG_ROWS = 80
+MAIN_UNROLL = 8
+HALO_UNROLL = 8
 F32 = jnp.float32
 BF16 = jnp.bfloat16
 
@@ -25,18 +27,60 @@
     return result
 
 
-def render_kernel(table, tiles, out, wide):
+def render_kernel(
+    owner, source, tops, lefts, codes, tiles, out, landing, wide, found, table, arrived, listed
+):
     parts = out.shape[0]
     sections = tiles.shape[0]
+    copies = [
+        pltpu.make_async_copy(tiles.at[z], landing.at[z], arrived.at[z]) for z in range(sections)
+    ]
+    for copy in copies:
+        copy.start()
+
+    me = lax.axis_index("xy")
+    mine = jnp.int32(0)
+    for k in range(parts):
+        mine = jnp.where(owner[k] == me, k, mine)
+    count = source.shape[2]
+    blank = jnp.full((8 - sections, count), -1, jnp.int32)
+    match = jnp.concatenate([source[z] for z in range(sections)] + [blank], axis=0) == mine
+    within = iota((8, count), 1) & 31
+    rank = match.astype(jnp.int32)
+    for reach in (1, 2, 4, 8, 16):
+        rank = rank + jnp.where(within >= reach, pltpu.roll(rank, reach, 1), 0)
+    packed = tops[...] + (lefts[...] << 9) + (codes[...] << 18)
+    packed = jnp.concatenate([packed, blank], axis=0)
+    pieces = []
+    for slot in range(2):
+        chosen = jnp.where(jnp.logical_and(match, rank == slot + 1), packed, 0)
+        for k in range(3):
+            pieces.append(((chosen >> (8 * k)) & 255).astype(F32))
+    strips = (iota((count, 128), 0) // 32 == iota((count, 128), 1)).astype(F32).astype(BF16)
+    sums = jnp.dot(
+        jnp.concatenate(pieces, axis=0).astype(BF16), strips, preferred_element_type=F32
+    ).astype(jnp.int32)
+    pair = [
+        sums[24 * slot : 24 * slot + 8]
+        + (sums[24 * slot + 8 : 24 * slot + 16] << 8)
+        + (sums[24 * slot + 16 : 24 * slot + 24] << 16)
+        for slot in range(2)
+    ]
+    found[...] = jnp.where(iota((8, 128), 0) < 2, pair[0], pltpu.roll(pair[1], 2, 0))
+    listing = pltpu.make_async_copy(found, table, listed.at[0])
+    listing.start()
+
     for z in range(sections):
+        copies[z].wait()
         for t in range(4):
-            wide[z, t] = tiles[z, :, 128 * t : 128 * t + 128].astype(F32)
+            wide[z, t] = landing[z, :, 128 * t : 128 * t + 128].astype(F32)
+    listing.wait()
     lane = iota((8, 128), 1)
     group = lane // 32
     lane_tall = iota((SUB, 128), 1)
 
     def one(q, z, slot):
-        code = table[(z * parts + q) * 2 + slot]
+        code = table[2 * slot + z, q]
         y = code & 511
         x = (code >> 9) & 511
         a = ((code >> 20) & 3).astype(F32) * 0.25
@@ -58,7 +102,7 @@
         value = (1.0 - b) * by_index(group, here) + b * by_index(group, right)
         out[q, z * 2 + slot] = value.astype(BF16)
 
-    @pl.loop(0, parts)
+    @pl.loop(0, parts, unroll=MAIN_UNROLL)
     def _(q):
         for z in range(sections):
             for slot in range(2):
@@ -67,7 +111,7 @@
     sub = iota((8, 128), 0)
     which = jnp.where(sub < 4, group, (group + 1) & 3)
 
-    @pl.loop(0, parts)
+    @pl.loop(0, parts, unroll=HALO_UNROLL)
     def _(q):
         after = jnp.minimum(q + 1, parts - 1)
         before = jnp.maximum(q - 1, 0)
@@ -142,16 +186,21 @@
     two[...] = total.astype(BF16)
 
 
-def conv_kernel(flags, bias_two, bias_one, before, own, after, one, two, out, shifted, hidden):
+def conv_kernel(flags, bias_one, bias_two, before, own, after, one, two, out, shifted, hidden):
     lane = iota((IMG_ROWS, W), 1)
     for number, (ref, z) in enumerate(
         [(before, 0), (before, 1), (own, 0), (own, 1), (after, 0), (after, 1)]
     ):
         plane = ref[z].astype(F32)
+        if number < 2:
+            plane = jnp.where(flags[2] == 0, 0.0, plane)
+        if number >= 4:
+            plane = jnp.where(flags[3] == 0, 0.0, plane)
         shifted[number, 0] = jnp.where(lane == 0, 0.0, pltpu.roll(plane, 1, 1))
         shifted[number, 1] = plane
         shifted[number, 2] = jnp.where(lane == W - 1, 0.0, pltpu.roll(plane, W - 1, 1))
-    gain = bias_one[...][:, :1]
+    row = iota((8, W), 0)
+    gain = by_index(row, [bias_one[o] for o in range(8)])
     height = HID_ROWS * 8
     row = iota((height, W), 0)
     for p in range(4):
@@ -224,26 +273,31 @@
     deep = lax.axis_index("gz")
     sections = raw_tiles.shape[0]
     source = src_tile.reshape(sections, parts, 32)
-    packed = (shift_y + (shift_x << 9) + (subpixel << 18)).reshape(sections, parts, 32)
     tile_ids = jnp.arange(parts, dtype=jnp.int32)
-    mine = jnp.sum(jnp.where(owner_map == me, tile_ids, 0))
     number = jnp.arange(32, dtype=jnp.int32)
-    match = source == mine
-    first = jnp.min(jnp.where(match, number, 31), axis=-1)
-    last = jnp.max(jnp.where(match, number, 0), axis=-1)
-    chosen = jnp.stack([first, last], axis=-1)
-    table = jnp.sum(
-        jnp.where(chosen[..., None] == number, packed[:, :, None, :], 0), axis=-1
-    ).reshape(-1)
 
     outgoing = pl.pallas_call(
         render_kernel,
         out_shape=jax.ShapeDtypeStruct((parts, 5, 8, 128), BF16),
-        in_specs=[smem(), vmem()],
+        in_specs=[smem()] + [vmem()] * 4 + [pl.BlockSpec(memory_space=pl.ANY)],
         out_specs=vmem(),
-        scratch_shapes=[pltpu.VMEM((sections, 4, 512, 128), F32)],
+        scratch_shapes=[
+            pltpu.VMEM((sections, 512, 512), BF16),
+            pltpu.VMEM((sections, 4, 512, 128), F32),
+            pltpu.VMEM((8, 128), jnp.int32),
+            pltpu.SMEM((8, 128), jnp.int32),
+            pltpu.SemaphoreType.DMA((sections,)),
+            pltpu.SemaphoreType.DMA((1,)),
+        ],
         name="render",
-    )(table, raw_tiles.reshape(sections, 512, 512))
+    )(
+        owner_map,
+        src_tile.reshape(sections, 1, parts * 32),
+        shift_y,
+        shift_x,
+        subpixel,
+        raw_tiles.reshape(sections, 512, 512),
+    )
 
     received = lax.all_to_all(outgoing, "xy", split_axis=0, concat_axis=0, tiled=True)
 
@@ -263,17 +317,6 @@
     )
     places = (holder * 2 + second.astype(jnp.int32)).reshape(-1)
     flags = jnp.stack([me > 0, me < parts - 1, deep > 0, deep < depth - 1]).astype(jnp.int32)
-
-    image = pl.pallas_call(
-        assemble_kernel,
-        out_shape=jax.ShapeDtypeStruct((sections, IMG_ROWS, W), BF16),
-        in_specs=[smem(), smem(), vmem()],
-        out_specs=vmem(),
-        name="assemble",
-    )(places, flags, received)
-
-    before = lax.ppermute(image, "gz", [(i, i + 1) for i in range(depth - 1)])
-    after = lax.ppermute(image, "gz", [(i + 1, i) for i in range(depth - 1)])
 
     banded_one, banded_two = pl.pallas_call(
         band_kernel,
@@ -286,10 +329,24 @@
         name="bands",
     )(weight_one.reshape(8, 27), weight_two.reshape(8, 216))
 
+    received, places, flags, banded_one, banded_two = lax.optimization_barrier(
+        (received, places, flags, banded_one, banded_two)
+    )
+    image = pl.pallas_call(
+        assemble_kernel,
+        out_shape=jax.ShapeDtypeStruct((sections, IMG_ROWS, W), BF16),
+        in_specs=[smem(), smem(), vmem()],
+        out_specs=vmem(),
+        name="assemble",
+    )(places, flags, received)
+
+    before = lax.ppermute(image, "gz", [(i, (i + 1) % depth) for i in range(depth)])
+    after = lax.ppermute(image, "gz", [((i + 1) % depth, i) for i in range(depth)])
+
     return pl.pallas_call(
         conv_kernel,
         out_shape=jax.ShapeDtypeStruct((8, sections, 64, W), BF16),
-        in_specs=[smem(), smem()] + [vmem()] * 6,
+        in_specs=[smem()] * 3 + [vmem()] * 5,
         out_specs=vmem(),
         scratch_shapes=[
             pltpu.VMEM((6, 3, IMG_ROWS, W), F32),
@@ -298,8 +355,8 @@
         name="convolve",
     )(
         flags,
+        bias_one,
         bias_two,
-        jnp.broadcast_to(bias_one[:, None], (8, 128)),
         before,
         image,
         after,

time: 59.2 us -> 49.5 us (0.84)
  starting transfers between devices: 23.4 us -> 19.6 us
  waiting for transfers between devices: 8.16 us -> 5.73 us
  other arithmetic: 3.74 us -> 1.36 us
  Pallas kernels: 17.4 us -> 16.1 us
    all_to_all x1, waiting for transfers between devices: 8.16 us -> 2.52 us  [on_device(): lax.all_to_all(outgoing, 'xy', split_axis=0, concat_axis=0, tiled=True)]
    ppermute x2, starting transfers between devices: 10.5 us -> 6.73 us  [the longest x1 4.34 us: on_device(): lax.ppermute(image, 'gz', [((i + 1) % depth, i) for i in range(depth)])]
    ppermute x2, waiting for transfers between devices: 0.01 us -> 3.21 us  [the longest x1 3.21 us: on_device(): lax.ppermute(image, 'gz', [((i + 1) % depth, i) for i in range(depth)])]
    unnamed x21 -> x15, local copies, waits for them, and re-layouts: 2.09 us -> 4.06 us
    pallas_call x1, Pallas kernels: 8.35 us -> 7.02 us  [on_device(): pl.pallas_call(render_kernel, out_shape=jax.ShapeDtypeStruct((parts, 5, 8...]
    reduce_sum x2 -> x0, other arithmetic: 0.85 us -> none  [the longest x1 0.63 us: on_device(): mine = jnp.sum(jnp.where(owner_map == me, tile_ids, 0))]
    reduce_min x1 -> x0, other arithmetic: 0.82 us -> none  [on_device(): first = jnp.min(jnp.where(match, number, 31), axis=-1)]
    broadcast_in_dim x2 -> x0, local copies, waits for them, and re-layouts: 0.75 us -> none  [the longest x1 0.66 us: on_device(): jnp.broadcast_to(bias_one[:, None], (8, 128))]
  transfers between devices with their start and end apart: 3 -> 3, of which waited for: 1 -> 2; matrix products, arithmetic and copies ran while one was open for 6% -> 7% of each run, Pallas kernels for 4% -> 4%
where the time goes in v2:
time: 49.5 us; the launch traced here: 49.1 us
  starting transfers between devices  19.6 us (40%)
  Pallas kernels  16.1 us (33%)
  local copies, waits for them, and re-layouts  6.16 us (12%)
  waiting for transfers between devices  5.73 us (12%)
  other arithmetic  1.36 us (3%)
    all_to_all x1, starting transfers between devices, on_device(): lax.all_to_all(outgoing, 'xy', split_axis=0, concat_axis=0, tiled=True)  12.9 us
    pallas_call x1, Pallas kernels, on_device(): pl.pallas_call(render_kernel, out_shape=jax.ShapeDtypeStruct((parts, 5, 8...  7.02 us
    pallas_call x1, Pallas kernels, on_device(): pl.pallas_call(conv_kernel, out_shape=jax.ShapeDtypeStruct((8, sections,...  4.97 us
    ppermute x1, starting transfers between devices, on_device(): lax.ppermute(image, 'gz', [((i + 1) % depth, i) for i in range(depth)])  4.34 us
    unnamed x15, local copies, waits for them, and re-layouts  4.06 us
    ppermute x1, waiting for transfers between devices, on_device(): lax.ppermute(image, 'gz', [((i + 1) % depth, i) for i in range(depth)])  3.21 us
    all_to_all x1, waiting for transfers between devices, on_device(): lax.all_to_all(outgoing, 'xy', split_axis=0, concat_axis=0, tiled=True)  2.52 us
    ppermute x1, starting transfers between devices, on_device(): lax.ppermute(image, 'gz', [(i, (i + 1) % depth) for i in range(depth)])  2.39 us
  transfers between devices with their start and end apart: 3, of which 2 were waited for; matrix products, arithmetic and copies ran while one was open for 7% of the time, Pallas kernels for 4%

profile of v2, /device:TPU:25, one launch (start us, length us, event | category | flops | bytes accessed | tf_op | source)
XLA Modules:
  0.0 49.1 jit_solution(939181076230091181)
XLA Ops:
  0.0 7.0 %render.1 = bf16[32,5,8,128]{3,2,1,0:T(8,128)(2,1)} custom-call(s32[32]{0:T(128)} %owner.1, s32[2,1,1024]{2,1,0:T(1,128)} %bitcast.11, s32[2,1024]{1,0:T(2,128)} %tops.1, s32[2,1024]{1,0:T(2,128)} %lefts.1, s32[2,1024]{1,0:T(2,128)} %codes.1, bf16[2,512,512]{2,1,0:T(8,128)(2,1)} %bitcast.10), custom_call_target="tpu_custom_call" | custom-call | tf_op jit(solution)/shard_map/render/pallas_call | solution.py:279
  7.0 12.9 %all-to-all-start = ((bf16[32,5,8,128]{3,2,1,0:T(8,128)(2,1)}), bf16[32,5,8,128]{3,2,1,0:T(8,128)(2,1)S(1)}, u32[]{:S(2)}, u32[]{:S(2)}) async-start(bf16[32,5,8,128]{3,2,1,0:T(8,128)(2,1)} %render.1), calls=%async_computation | async-start | bytes 655360 | tf_op jit(solution)/shard_map/all_to_all | solution.py:302
  19.9 0.0 copy-start.4
  20.0 0.7 %copy-done.4 = s32[2,1024,1]{1,2,0:T(1,128)S(1)} copy-done((s32[2,1024,1]{1,2,0:T(1,128)S(1)}, s32[2,1024,1]{1,2,0:T(1,128)}, u32[]{:S(2)}) %copy-start.4) | copy-done | bytes 8216
  20.7 0.0 copy-start.5
  20.7 0.1 iota_compare_fusion.2
  20.8 0.6 %copy-done.5 = bf16[8,1,3,3,3]{0,4,3,2,1:T(4,128)(2,1)S(1)} copy-done((bf16[8,1,3,3,3]{0,4,3,2,1:T(4,128)(2,1)S(1)}, bf16[8,1,3,3,3]{0,4,3,2,1:T(4,128)(2,1)}, u32[]{:S(2)}) %copy-start.5) | copy-done | bytes 456
  21.4 0.6 %copy.17.flat_one = bf16[8,27]{1,0:T(8,128)(2,1)} copy(bf16[8,27]{0,1:T(8,128)(2,1)S(1)} %reshape.68) | data formatting | bytes 864 | tf_op jit(solution)/shard_map/reshape | solution.py:330
  22.0 0.0 copy-start.3
  22.0 0.1 broadcast_in_dim.38
  22.1 0.1 select_reduce_fusion.1
  22.2 0.0 copy-start.6
  22.3 0.6 %copy-done.6 = s32[32]{0:T(128)S(1)} copy-done((s32[32]{0:T(128)S(1)}, s32[32]{0:T(128)}, u32[]{:S(2)}) %copy-start.6) | copy-done | bytes 152
  22.9 0.3 select_reduce_fusion
  23.1 0.3 and_reduce_fusion
  23.4 0.6 %add.28.table = s32[192]{0:T(256)} reshape(s32[2,3,32]{2,1,0:T(4,128)S(1)} %convert_add_fusion) | data formatting | bytes 1536 | tf_op jit(solution)/shard_map/add | solution.py:318
  24.1 0.0 copy-done.3
  24.1 0.1 copy.16
  24.2 0.7 %copy.18.flat_two = bf16[8,216]{1,0:T(8,128)(2,1)} copy(bf16[8,216]{0,1:T(8,128)(2,1)S(1)} %reshape.69) | data formatting | bytes 6912 | tf_op jit(solution)/shard_map/reshape | solution.py:330
  24.9 2.1 %bands.1 = (bf16[176,216]{1,0:T(8,128)(2,1)}, bf16[192,240]{1,0:T(8,128)(2,1)}) custom-call(bf16[8,27]{1,0:T(8,128)(2,1)} %copy.17.flat_one, bf16[8,216]{1,0:T(8,128)(2,1)} %copy.18.flat_two), custom_call_target="tpu_custom_call" | custom-call | tf_op jit(solution)/shard_map/bands/pallas_call | solution.py:321
  27.0 0.6 %add_convert_fusion.flags = s32[4]{0:T(128)} fusion(pred[1]{0:T(512)(128)(4,1)} %bitcast.5, pred[1]{0:T(512)(128)(4,1)} %bitcast.4, pred[1]{0:T(512)(128)(4,1)} %bitcast.3, pred[1]{0:T(512)(128)(4,1)} %bitcast.2), kind=kLoop, calls=%fused_computation.7 | loop fusion | flops 16 | bytes 20 | tf_op jit(solution)/shard_map/convert_element_type | solution.py:319
  27.6 2.5 %all-to-all-done.pool = bf16[32,5,8,128]{3,2,1,0:T(8,128)(2,1)S(1)} async-done(((bf16[32,5,8,128]{3,2,1,0:T(8,128)(2,1)}), bf16[32,5,8,128]{3,2,1,0:T(8,128)(2,1)S(1)}, u32[]{:S(2)}, u32[]{:S(2)}) %all-to-all-start) | async-done | bytes 327712 | tf_op jit(solution)/shard_map/all_to_all | solution.py:302
  30.1 0.0 copy-start
  30.1 0.7 %copy-done = bf16[32,5,8,128]{3,2,1,0:T(8,128)(2,1)} copy-done((bf16[32,5,8,128]{3,2,1,0:T(8,128)(2,1)}, bf16[32,5,8,128]{3,2,1,0:T(8,128)(2,1)S(1)}, u32[]{:S(2)}) %copy-start) | copy-done | bytes 327704
  30.8 2.0 %assemble.1.own = bf16[2,80,512]{2,1,0:T(8,128)(2,1)} custom-call(s32[192]{0:T(256)} %add.28.table, s32[4]{0:T(128)} %add_convert_fusion.flags, bf16[32,5,8,128]{3,2,1,0:T(8,128)(2,1)} %copy-done), custom_call_target="tpu_custom_call" | custom-call | tf_op jit(solution)/shard_map/assemble/pallas_call | solution.py:335
  32.8 4.3 %collective-permute-start.1 = (bf16[2,80,512]{2,1,0:T(8,128)(2,1)}, bf16[2,80,512]{2,1,0:T(8,128)(2,1)S(1)}, u32[]{:S(2)}, u32[]{:S(2)}) collective-permute-start(bf16[2,80,512]{2,1,0:T(8,128)(2,1)} %assemble.1.own), channel_id=1, source_target_pairs={{1,0},{2,1},{3,2},{4,3},{5,4},{6,5},{7,6},{8,7},{9,8},{10,9},{11,1... | collective-permute-start | bytes 491528 | tf_op jit(solution)/shard_map/ppermute | solution.py:344
  37.2 2.4 %collective-permute-start = (bf16[2,80,512]{2,1,0:T(8,128)(2,1)}, bf16[2,80,512]{2,1,0:T(8,128)(2,1)S(1)}, u32[]{:S(2)}, u32[]{:S(2)}) collective-permute-start(bf16[2,80,512]{2,1,0:T(8,128)(2,1)} %assemble.1.own), channel_id=1, source_target_pairs={{0,1},{1,2},{2,3},{3,4},{4,5},{5,6},{6,7},{7,8},{8,9},{9,10},{10,1... | collective-permute-start | bytes 491528 | tf_op jit(solution)/shard_map/ppermute | solution.py:343
  39.6 3.2 %collective-permute-done.1.after = bf16[2,80,512]{2,1,0:T(8,128)(2,1)S(1)} collective-permute-done((bf16[2,80,512]{2,1,0:T(8,128)(2,1)}, bf16[2,80,512]{2,1,0:T(8,128)(2,1)S(1)}, u32[]{:S(2)}, u32[]{:S(2)}) %collective-permute-start.1) | collective-permute-done | bytes 163872 | tf_op jit(solution)/shard_map/ppermute | solution.py:344
  42.8 0.0 copy-start.1
  42.8 0.0 collective-permute-done.before
  42.8 0.7 %copy-done.1 = bf16[2,80,512]{2,1,0:T(8,128)(2,1)} copy-done((bf16[2,80,512]{2,1,0:T(8,128)(2,1)}, bf16[2,80,512]{2,1,0:T(8,128)(2,1)S(1)}, u32[]{:S(2)}) %copy-start.1) | copy-done | bytes 163864
  43.4 0.0 copy-start.2
  43.4 0.7 %copy-done.2 = bf16[2,80,512]{2,1,0:T(8,128)(2,1)} copy-done((bf16[2,80,512]{2,1,0:T(8,128)(2,1)}, bf16[2,80,512]{2,1,0:T(8,128)(2,1)S(1)}, u32[]{:S(2)}) %copy-start.2) | copy-done | bytes 163864
  44.1 5.0 %convolve.1 = bf16[8,2,64,512]{3,2,1,0:T(8,128)(2,1)} custom-call(s32[4]{0:T(128)} %add_convert_fusion.flags, f32[8]{0:T(128)} %bias_one.1, f32[8]{0:T(128)} %bias_two.1, bf16[2,80,512]{2,1,0:T(8,128)(2,1)} %copy-done.2, bf16[2,80,512]{2,1,0:T(8,128)(2,1)} %assemble.1.own, bf16[2,80,512]{2,1,0:T(8,128)(2,1)} %copy-done.1, ...), custom_call_target="tpu_custom_call" | custom-call | tf_op jit(solution)/shard_map/convolve/pallas_call | solution.py:346
  (6 shorter events, 0.1 us)
Async XLA Ops:
  7.0 23.1 %all-to-all-start = ((bf16[32,5,8,128]{3,2,1,0:T(8,128)(2,1)}), bf16[32,5,8,128]{3,2,1,0:T(8,128)(2,1)S(1)}, u32[]{:S(2)}, u32[]{:S(2)}) async-start(bf16[32,5,8,128]{3,2,1,0:T(8,128)(2,1)} %render.1), calls=%async_computation | async-start | bytes 655360 | tf_op jit(solution)/shard_map/all_to_all | solution.py:302
  19.9 0.7 %copy-start.4 = (s32[2,1024,1]{1,2,0:T(1,128)S(1)}, s32[2,1024,1]{1,2,0:T(1,128)}, u32[]{:S(2)}) copy-start(s32[2,1024,1]{1,2,0:T(1,128)} %param.11) | copy-start | bytes 24580
  20.7 0.7 %copy-start.5 = (bf16[8,1,3,3,3]{0,4,3,2,1:T(4,128)(2,1)S(1)}, bf16[8,1,3,3,3]{0,4,3,2,1:T(4,128)(2,1)}, u32[]{:S(2)}) copy-start(bf16[8,1,3,3,3]{0,4,3,2,1:T(4,128)(2,1)} %param.16) | copy-start | bytes 1300
  22.0 2.0 %copy-start.3 = (bf16[8,8,3,3,3]{1,0,4,3,2:T(8,128)(2,1)S(1)}, bf16[8,8,3,3,3]{1,0,4,3,2:T(8,128)(2,1)}, u32[]{:S(2)}) copy-start(bf16[8,8,3,3,3]{1,0,4,3,2:T(8,128)(2,1)} %param.18) | copy-start | bytes 10372
  22.2 0.7 %copy-start.6 = (s32[32]{0:T(128)S(1)}, s32[32]{0:T(128)}, u32[]{:S(2)}) copy-start(s32[32]{0:T(128)} %owner.1) | copy-start | bytes 388
  30.1 0.7 %copy-start = (bf16[32,5,8,128]{3,2,1,0:T(8,128)(2,1)}, bf16[32,5,8,128]{3,2,1,0:T(8,128)(2,1)S(1)}, u32[]{:S(2)}) copy-start(bf16[32,5,8,128]{3,2,1,0:T(8,128)(2,1)S(1)} %all-to-all-done.pool) | copy-start | bytes 983044
  32.8 9.9 %collective-permute-start.1 = (bf16[2,80,512]{2,1,0:T(8,128)(2,1)}, bf16[2,80,512]{2,1,0:T(8,128)(2,1)S(1)}, u32[]{:S(2)}, u32[]{:S(2)}) collective-permute-start(bf16[2,80,512]{2,1,0:T(8,128)(2,1)} %assemble.1.own), channel_id=1, source_target_pairs={{1,0},{2,1},{3,2},{4,3},{5,4},{6,5},{7,6},{8,7},{9,8},{10,9},{11,1... | collective-permute-start | bytes 491528 | tf_op jit(solution)/shard_map/ppermute | solution.py:344
  37.2 5.6 %collective-permute-start = (bf16[2,80,512]{2,1,0:T(8,128)(2,1)}, bf16[2,80,512]{2,1,0:T(8,128)(2,1)S(1)}, u32[]{:S(2)}, u32[]{:S(2)}) collective-permute-start(bf16[2,80,512]{2,1,0:T(8,128)(2,1)} %assemble.1.own), channel_id=1, source_target_pairs={{0,1},{1,2},{2,3},{3,4},{4,5},{5,6},{6,7},{7,8},{8,9},{9,10},{10,1... | collective-permute-start | bytes 491528 | tf_op jit(solution)/shard_map/ppermute | solution.py:343
  42.8 0.7 %copy-start.1 = (bf16[2,80,512]{2,1,0:T(8,128)(2,1)}, bf16[2,80,512]{2,1,0:T(8,128)(2,1)S(1)}, u32[]{:S(2)}) copy-start(bf16[2,80,512]{2,1,0:T(8,128)(2,1)S(1)} %collective-permute-done.1.after) | copy-start | bytes 491524
  43.4 0.7 %copy-start.2 = (bf16[2,80,512]{2,1,0:T(8,128)(2,1)}, bf16[2,80,512]{2,1,0:T(8,128)(2,1)S(1)}, u32[]{:S(2)}) copy-start(bf16[2,80,512]{2,1,0:T(8,128)(2,1)S(1)} %collective-permute-done.before) | copy-start | bytes 491524

commit v3 on v2

--- a/solution.py
+++ b/solution.py
@@ -186,7 +186,9 @@
     two[...] = total.astype(BF16)
 
 
-def conv_kernel(flags, bias_one, bias_two, before, own, after, one, two, out, shifted, hidden):
+def conv_kernel(
+    flags, bias_one, bias_two, before, own, after, one, two, out, shifted, hidden, stage, sent
+):
     lane = iota((IMG_ROWS, W), 1)
     for number, (ref, z) in enumerate(
         [(before, 0), (before, 1), (own, 0), (own, 1), (after, 0), (after, 1)]
@@ -231,6 +233,7 @@
         hidden[3] = jnp.zeros(hidden.shape[1:], BF16)
 
     edge = iota((64, W), 1)
+    copies = []
     for z in range(2):
         for pair in range(4):
             halves = []
@@ -242,9 +245,17 @@
                 left = jnp.where(edge == 0, 0.0, pltpu.roll(total[0:64], 1, 1))
                 right = jnp.where(edge == W - 1, 0.0, pltpu.roll(total[128:192], W - 1, 1))
                 halves.append(total[64:128] + left + right)
+            rows = pl.ds(16 * pair, 16)
             for o in range(8):
                 both = jnp.concatenate([half[8 * o : 8 * o + 8] for half in halves], axis=0)
-                out[o, z, 16 * pair : 16 * pair + 16, :] = (both + bias_two[o]).astype(BF16)
+                stage[o, z, rows, :] = (both + bias_two[o]).astype(BF16)
+            copy = pltpu.make_async_copy(
+                stage.at[:, z, rows, :], out.at[:, z, rows, :], sent.at[4 * z + pair]
+            )
+            copy.start()
+            copies.append(copy)
+    for copy in copies:
+        copy.wait()
 
 
 def smem():
@@ -253,6 +264,14 @@
 
 def vmem():
     return pl.BlockSpec(memory_space=pltpu.VMEM)
+
+
+def in_vmem(array):
+    return pltpu.with_memory_space_constraint(array, pltpu.VMEM)
+
+
+def in_smem(array):
+    return pltpu.with_memory_space_constraint(array, pltpu.SMEM)
 
 
 def on_device(
@@ -278,7 +297,7 @@
 
     outgoing = pl.pallas_call(
         render_kernel,
-        out_shape=jax.ShapeDtypeStruct((parts, 5, 8, 128), BF16),
+        out_shape=pltpu.VMEM((parts, 5, 8, 128), BF16),
         in_specs=[smem()] + [vmem()] * 4 + [pl.BlockSpec(memory_space=pl.ANY)],
         out_specs=vmem(),
         scratch_shapes=[
@@ -321,8 +340,8 @@
     banded_one, banded_two = pl.pallas_call(
         band_kernel,
         out_shape=(
-            jax.ShapeDtypeStruct((HID_ROWS * 8, 9 * WIN_ROWS), BF16),
-            jax.ShapeDtypeStruct((192, 240), BF16),
+            pltpu.VMEM((HID_ROWS * 8, 9 * WIN_ROWS), BF16),
+            pltpu.VMEM((192, 240), BF16),
         ),
         in_specs=[vmem(), vmem()],
         out_specs=(vmem(), vmem()),
@@ -334,11 +353,11 @@
     )
     image = pl.pallas_call(
         assemble_kernel,
-        out_shape=jax.ShapeDtypeStruct((sections, IMG_ROWS, W), BF16),
+        out_shape=pltpu.VMEM((sections, IMG_ROWS, W), BF16),
         in_specs=[smem(), smem(), vmem()],
         out_specs=vmem(),
         name="assemble",
-    )(places, flags, received)
+    )(in_smem(places), in_smem(flags), in_vmem(received))
 
     before = lax.ppermute(image, "gz", [(i, (i + 1) % depth) for i in range(depth)])
     after = lax.ppermute(image, "gz", [((i + 1) % depth, i) for i in range(depth)])
@@ -347,21 +366,23 @@
         conv_kernel,
         out_shape=jax.ShapeDtypeStruct((8, sections, 64, W), BF16),
         in_specs=[smem()] * 3 + [vmem()] * 5,
-        out_specs=vmem(),
+        out_specs=pl.BlockSpec(memory_space=pl.ANY),
         scratch_shapes=[
             pltpu.VMEM((6, 3, IMG_ROWS, W), F32),
             pltpu.VMEM((4, 66 * 8, W), BF16),
+            pltpu.VMEM((8, sections, 64, W), BF16),
+            pltpu.SemaphoreType.DMA((4 * sections,)),
         ],
         name="convolve",
     )(
-        flags,
+        in_smem(flags),
         bias_one,
         bias_two,
-        before,
-        image,
-        after,
-        banded_one,
-        banded_two,
+        in_vmem(before),
+        in_vmem(image),
+        in_vmem(after),
+        in_vmem(banded_one),
+        in_vmem(banded_two),
     )
 
 

time: 49.5 us -> 46.2 us (0.933)
  the two profiles are of different devices: /device:TPU:25 before, /device:TPU:64 now
where the time goes in v3:
time: 46.2 us; the launch traced here: 45.7 us
  Pallas kernels  13.8 us (30%)
  starting transfers between devices  13.8 us (30%)
  waiting for transfers between devices  12.4 us (27%)
  local copies, waits for them, and re-layouts  4.17 us (9%)
  other arithmetic  1.44 us (3%)
    all_to_all x1, starting transfers between devices, on_device(): lax.all_to_all(outgoing, 'xy', split_axis=0, concat_axis=0, tiled=True)  12.6 us
    pallas_call x1, Pallas kernels, on_device(): pl.pallas_call(render_kernel, out_shape=pltpu.VMEM((parts, 5, 8, 128), BF...  7.02 us
    all_to_all x1, waiting for transfers between devices, on_device(): lax.all_to_all(outgoing, 'xy', split_axis=0, concat_axis=0, tiled=True)  6.44 us
    pallas_call x1, Pallas kernels, on_device(): pl.pallas_call(conv_kernel, out_shape=jax.ShapeDtypeStruct((8, sections,...  4.28 us
    ppermute x1, waiting for transfers between devices, on_device(): lax.ppermute(image, 'gz', [(i, (i + 1) % depth) for i in range(depth)])  3.12 us
    ppermute x1, waiting for transfers between devices, on_device(): lax.ppermute(image, 'gz', [((i + 1) % depth, i) for i in range(depth)])  2.83 us
    unnamed x9, local copies, waits for them, and re-layouts  2.03 us
    pallas_call x1, Pallas kernels, on_device(): pl.pallas_call(band_kernel, out_shape=(pltpu.VMEM((HID_ROWS * 8, 9 * WIN_...  1.45 us
  transfers between devices with their start and end apart: 3, of which 3 were waited for; matrix products, arithmetic and copies ran while one was open for 8% of the time, Pallas kernels for 3%

profile of v3, /device:TPU:64, one launch (start us, length us, event | category | flops | bytes accessed | tf_op | source)
XLA Modules:
  0.0 45.7 jit_solution(9515101989989903050)
XLA Ops:
  0.0 7.0 %render.1 = bf16[32,5,8,128]{3,2,1,0:T(8,128)(2,1)} custom-call(s32[32]{0:T(128)} %owner.1, s32[2,1,1024]{2,1,0:T(1,128)} %bitcast.11, s32[2,1024]{1,0:T(2,128)} %tops.1, s32[2,1024]{1,0:T(2,128)} %lefts.1, s32[2,1024]{1,0:T(2,128)} %codes.1, bf16[2,512,512]{2,1,0:T(8,128)(2,1)} %bitcast.10), custom_call_target="tpu_custom_call" | custom-call | tf_op jit(solution)/shard_map/render/pallas_call | solution.py:298
  7.0 12.6 %all-to-all-start = ((bf16[32,5,8,128]{3,2,1,0:T(8,128)(2,1)}), bf16[32,5,8,128]{3,2,1,0:T(8,128)(2,1)S(1)}, u32[]{:S(2)}, u32[]{:S(2)}) async-start(bf16[32,5,8,128]{3,2,1,0:T(8,128)(2,1)} %render.1), calls=%async_computation | async-start | bytes 655360 | tf_op jit(solution)/shard_map/all_to_all | solution.py:321
  19.6 0.0 copy-start.1
  19.7 0.7 %copy-done.1 = s32[2,1024,1]{1,2,0:T(1,128)S(1)} copy-done((s32[2,1024,1]{1,2,0:T(1,128)S(1)}, s32[2,1024,1]{1,2,0:T(1,128)}, u32[]{:S(2)}) %copy-start.1) | copy-done | bytes 8216
  20.4 0.0 copy-start.2
  20.4 0.1 iota_compare_fusion.2
  20.5 0.6 %copy-done.2 = bf16[8,1,3,3,3]{0,4,3,2,1:T(4,128)(2,1)S(1)} copy-done((bf16[8,1,3,3,3]{0,4,3,2,1:T(4,128)(2,1)S(1)}, bf16[8,1,3,3,3]{0,4,3,2,1:T(4,128)(2,1)}, u32[]{:S(2)}) %copy-start.2) | copy-done | bytes 456
  21.1 0.7 %copy.17.flat_one = bf16[8,27]{1,0:T(8,128)(2,1)} copy(bf16[8,27]{0,1:T(8,128)(2,1)S(1)} %reshape.68) | data formatting | bytes 864 | tf_op jit(solution)/shard_map/reshape | solution.py:349
  21.8 0.0 copy-start
  21.8 0.1 broadcast_in_dim.38
  21.8 0.1 select_reduce_fusion.1
  21.9 0.0 copy-start.3
  22.0 0.6 %copy-done.3 = s32[32]{0:T(128)S(1)} copy-done((s32[32]{0:T(128)S(1)}, s32[32]{0:T(128)}, u32[]{:S(2)}) %copy-start.3) | copy-done | bytes 152
  22.6 0.3 select_reduce_fusion
  22.9 0.3 and_reduce_fusion
  23.2 0.7 %add.28.table = s32[192]{0:T(256)} reshape(s32[2,3,32]{2,1,0:T(4,128)S(1)} %convert_add_fusion) | data formatting | bytes 1536 | tf_op jit(solution)/shard_map/add | solution.py:337
  23.8 0.0 copy-done
  23.8 0.1 copy.16
  24.0 0.7 %copy.18.flat_two = bf16[8,216]{1,0:T(8,128)(2,1)} copy(bf16[8,216]{0,1:T(8,128)(2,1)S(1)} %reshape.69) | data formatting | bytes 6912 | tf_op jit(solution)/shard_map/reshape | solution.py:349
  24.6 1.5 %bands.1 = (bf16[176,216]{1,0:T(8,128)(2,1)S(1)}, bf16[192,240]{1,0:T(8,128)(2,1)S(1)}) custom-call(bf16[8,27]{1,0:T(8,128)(2,1)} %copy.17.flat_one, bf16[8,216]{1,0:T(8,128)(2,1)} %copy.18.flat_two), custom_call_target="tpu_custom_call" | custom-call | tf_op jit(solution)/shard_map/bands/pallas_call | solution.py:340
  26.1 0.7 %add_convert_fusion.flags = s32[4]{0:T(128)} fusion(pred[1]{0:T(512)(128)(4,1)} %bitcast.5, pred[1]{0:T(512)(128)(4,1)} %bitcast.4, pred[1]{0:T(512)(128)(4,1)} %bitcast.3, pred[1]{0:T(512)(128)(4,1)} %bitcast.2), kind=kLoop, calls=%fused_computation.7 | loop fusion | flops 16 | bytes 20 | tf_op jit(solution)/shard_map/convert_element_type | solution.py:338
  26.8 6.4 %all-to-all-done.pool = bf16[32,5,8,128]{3,2,1,0:T(8,128)(2,1)S(1)} async-done(((bf16[32,5,8,128]{3,2,1,0:T(8,128)(2,1)}), bf16[32,5,8,128]{3,2,1,0:T(8,128)(2,1)S(1)}, u32[]{:S(2)}, u32[]{:S(2)}) %all-to-all-start) | async-done | bytes 327712 | tf_op jit(solution)/shard_map/all_to_all | solution.py:321
  33.2 1.0 %assemble.1.own = bf16[2,80,512]{2,1,0:T(8,128)(2,1)S(1)} custom-call(s32[192]{0:T(256)} %add.28.table, s32[4]{0:T(128)} %add_convert_fusion.flags, bf16[32,5,8,128]{3,2,1,0:T(8,128)(2,1)S(1)} %all-to-all-done.pool), custom_call_target="tpu_custom_call" | custom-call | tf_op jit(solution)/shard_map/assemble/pallas_call | solution.py:354
  34.3 1.2 %collective-permute-start.1 = (bf16[2,80,512]{2,1,0:T(8,128)(2,1)S(1)}, bf16[2,80,512]{2,1,0:T(8,128)(2,1)S(1)}, u32[]{:S(2)}, u32[]{:S(2)}) collective-permute-start(bf16[2,80,512]{2,1,0:T(8,128)(2,1)S(1)} %assemble.1.own), channel_id=1, source_target_pairs={{1,0},{2,1},{3,2},{4,3},{5,4},{6,5},{7,6},{8,7},{9,8},{10,9},{11,1... | collective-permute-start | bytes 491528 | tf_op jit(solution)/shard_map/ppermute | solution.py:363
  35.4 0.0 collective-permute-start
  35.5 2.8 %collective-permute-done.1.after = bf16[2,80,512]{2,1,0:T(8,128)(2,1)S(1)} collective-permute-done((bf16[2,80,512]{2,1,0:T(8,128)(2,1)S(1)}, bf16[2,80,512]{2,1,0:T(8,128)(2,1)S(1)}, u32[]{:S(2)}, u32[]{:S(2)}) %collective-permute-start.1) | collective-permute-done | bytes 163872 | tf_op jit(solution)/shard_map/ppermute | solution.py:363
  38.3 3.1 %collective-permute-done.before = bf16[2,80,512]{2,1,0:T(8,128)(2,1)S(1)} collective-permute-done((bf16[2,80,512]{2,1,0:T(8,128)(2,1)S(1)}, bf16[2,80,512]{2,1,0:T(8,128)(2,1)S(1)}, u32[]{:S(2)}, u32[]{:S(2)}) %collective-permute-start) | collective-permute-done | bytes 163872 | tf_op jit(solution)/shard_map/ppermute | solution.py:362
  41.4 4.3 %convolve.1 = bf16[8,2,64,512]{3,2,1,0:T(8,128)(2,1)} custom-call(s32[4]{0:T(128)} %add_convert_fusion.flags, f32[8]{0:T(128)} %bias_one.1, f32[8]{0:T(128)} %bias_two.1, bf16[2,80,512]{2,1,0:T(8,128)(2,1)S(1)} %collective-permute-done.before, bf16[2,80,512]{2,1,0:T(8,128)(2,1)S(1)} %assemble.1.own, bf16[2,80,512]{2,1,0:T(8,128)(2,1)S(1)} %collective-permute-done.1.after, ...), custom_call_target="tpu_custom_call" | custom-call | tf_op jit(solution)/shard_map/convolve/pallas_call | solution.py:365
  (6 shorter events, 0.1 us)
Async XLA Ops:
  7.0 26.2 %all-to-all-start = ((bf16[32,5,8,128]{3,2,1,0:T(8,128)(2,1)}), bf16[32,5,8,128]{3,2,1,0:T(8,128)(2,1)S(1)}, u32[]{:S(2)}, u32[]{:S(2)}) async-start(bf16[32,5,8,128]{3,2,1,0:T(8,128)(2,1)} %render.1), calls=%async_computation | async-start | bytes 655360 | tf_op jit(solution)/shard_map/all_to_all | solution.py:321
  19.6 0.7 %copy-start.1 = (s32[2,1024,1]{1,2,0:T(1,128)S(1)}, s32[2,1024,1]{1,2,0:T(1,128)}, u32[]{:S(2)}) copy-start(s32[2,1024,1]{1,2,0:T(1,128)} %param.11) | copy-start | bytes 24580
  20.4 0.7 %copy-start.2 = (bf16[8,1,3,3,3]{0,4,3,2,1:T(4,128)(2,1)S(1)}, bf16[8,1,3,3,3]{0,4,3,2,1:T(4,128)(2,1)}, u32[]{:S(2)}) copy-start(bf16[8,1,3,3,3]{0,4,3,2,1:T(4,128)(2,1)} %param.16) | copy-start | bytes 1300
  21.8 2.0 %copy-start = (bf16[8,8,3,3,3]{1,0,4,3,2:T(8,128)(2,1)S(1)}, bf16[8,8,3,3,3]{1,0,4,3,2:T(8,128)(2,1)}, u32[]{:S(2)}) copy-start(bf16[8,8,3,3,3]{1,0,4,3,2:T(8,128)(2,1)} %param.18) | copy-start | bytes 10372
  21.9 0.7 %copy-start.3 = (s32[32]{0:T(128)S(1)}, s32[32]{0:T(128)}, u32[]{:S(2)}) copy-start(s32[32]{0:T(128)} %owner.1) | copy-start | bytes 388
  34.3 4.0 %collective-permute-start.1 = (bf16[2,80,512]{2,1,0:T(8,128)(2,1)S(1)}, bf16[2,80,512]{2,1,0:T(8,128)(2,1)S(1)}, u32[]{:S(2)}, u32[]{:S(2)}) collective-permute-start(bf16[2,80,512]{2,1,0:T(8,128)(2,1)S(1)} %assemble.1.own), channel_id=1, source_target_pairs={{1,0},{2,1},{3,2},{4,3},{5,4},{6,5},{7,6},{8,7},{9,8},{10,9},{11,1... | collective-permute-start | bytes 491528 | tf_op jit(solution)/shard_map/ppermute | solution.py:363
  35.4 6.0 %collective-permute-start = (bf16[2,80,512]{2,1,0:T(8,128)(2,1)S(1)}, bf16[2,80,512]{2,1,0:T(8,128)(2,1)S(1)}, u32[]{:S(2)}, u32[]{:S(2)}) collective-permute-start(bf16[2,80,512]{2,1,0:T(8,128)(2,1)S(1)} %assemble.1.own), channel_id=1, source_target_pairs={{0,1},{1,2},{2,3},{3,4},{4,5},{5,6},{6,7},{7,8},{8,9},{9,10},{10,1... | collective-permute-start | bytes 491528 | tf_op jit(solution)/shard_map/ppermute | solution.py:362

commit v4 on v3

--- a/solution.py
+++ b/solution.py
@@ -10,8 +10,11 @@
 HID_ROWS = 22
 WIN_ROWS = 24
 IMG_ROWS = 80
+BATCH = 8
 MAIN_UNROLL = 8
-HALO_UNROLL = 8
+HALO_UNROLL = 4
+UNROLL_ONE = 4
+UNROLL_TWO = 8
 F32 = jnp.float32
 BF16 = jnp.bfloat16
 
@@ -28,15 +31,57 @@
 
 
 def render_kernel(
-    owner, source, tops, lefts, codes, tiles, out, landing, wide, found, table, arrived, listed
+    owner_in,
+    source_in,
+    tops_in,
+    lefts_in,
+    codes_in,
+    tiles,
+    out,
+    owner,
+    source,
+    tops,
+    lefts,
+    codes,
+    landing,
+    wide,
+    kept,
+    ready,
+    found,
+    table,
+    arrived,
+    landed,
+    listed,
+    sent,
 ):
     parts = out.shape[0]
     sections = tiles.shape[0]
+    small = [
+        pltpu.make_async_copy(src, dst, arrived.at[n])
+        for n, (src, dst) in enumerate(
+            [
+                (source_in, source),
+                (owner_in, owner),
+                (tops_in, tops),
+                (lefts_in, lefts),
+                (codes_in, codes),
+            ]
+        )
+    ]
+    half = landing.shape[1] // 2
     copies = [
-        pltpu.make_async_copy(tiles.at[z], landing.at[z], arrived.at[z]) for z in range(sections)
+        pltpu.make_async_copy(
+            tiles.at[z, pl.ds(half * h, half), :],
+            landing.at[z, pl.ds(half * h, half), :],
+            landed.at[2 * z + h],
+        )
+        for z in range(sections)
+        for h in range(2)
     ]
-    for copy in copies:
+    for copy in small + copies:
         copy.start()
+    for copy in small:
+        copy.wait()
 
     me = lax.axis_index("xy")
     mine = jnp.int32(0)
@@ -71,13 +116,15 @@
     listing.start()
 
     for z in range(sections):
-        copies[z].wait()
-        for t in range(4):
-            wide[z, t] = landing[z, :, 128 * t : 128 * t + 128].astype(F32)
+        for h in range(2):
+            copies[2 * z + h].wait()
+            rows = pl.ds(half * h, half)
+            for t in range(4):
+                wide[z, t, rows, :] = landing[z, rows, 128 * t : 128 * t + 128].astype(F32)
     listing.wait()
     lane = iota((8, 128), 1)
     group = lane // 32
-    lane_tall = iota((SUB, 128), 1)
+    starts = lane % 32 == 0
 
     def one(q, z, slot):
         code = table[2 * slot + z, q]
@@ -88,38 +135,66 @@
         near = x >> 7
         far = jnp.minimum(near + 1, 3)
         low = x & 127
-        wraps = lane_tall < low
-        upper = jnp.where(wraps, wide[z, far, pl.ds(y, SUB), :], wide[z, near, pl.ds(y, SUB), :])
-        lower = jnp.where(
-            wraps, wide[z, far, pl.ds(y + 1, SUB), :], wide[z, near, pl.ds(y + 1, SUB), :]
-        )
-        mixed = (1.0 - a) * upper + a * lower
-        here, right = [], []
+        wraps = lane < low
+        here = []
         for g in range(4):
-            piece = mixed[8 * g : 8 * g + 8]
-            here.append(pltpu.roll(piece, (32 * g + 128 - low) & 127, 1))
-            right.append(pltpu.roll(piece, (32 * g + 127 - low) & 127, 1))
-        value = (1.0 - b) * by_index(group, here) + b * by_index(group, right)
-        out[q, z * 2 + slot] = value.astype(BF16)
-
-    @pl.loop(0, parts, unroll=MAIN_UNROLL)
-    def _(q):
-        for z in range(sections):
-            for slot in range(2):
-                one(q, z, slot)
+            upper = jnp.where(
+                wraps, wide[z, far, pl.ds(y + 8 * g, 8), :], wide[z, near, pl.ds(y + 8 * g, 8), :]
+            )
+            lower = jnp.where(
+                wraps,
+                wide[z, far, pl.ds(y + (8 * g + 1), 8), :],
+                wide[z, near, pl.ds(y + (8 * g + 1), 8), :],
+            )
+            mixed = (1.0 - a) * upper + a * lower
+            here.append(pltpu.roll(mixed, (32 * g + 128 - low) & 127, 1))
+        left = by_index(group, here)
+        spill = by_index(group, here[3:] + here[:3])
+        right = pltpu.roll(jnp.where(starts, spill, left), 127, 1)
+        value = (1.0 - b) * left + b * right
+        zs = z * 2 + slot
+        ready[q, zs] = value.astype(BF16)
+        kept[q, zs] = value if zs == 0 else pltpu.roll(value, 32 * zs, 1)
 
     sub = iota((8, 128), 0)
     which = jnp.where(sub < 4, group, (group + 1) & 3)
 
-    @pl.loop(0, parts, unroll=HALO_UNROLL)
-    def _(q):
-        after = jnp.minimum(q + 1, parts - 1)
-        before = jnp.maximum(q - 1, 0)
-        turned = []
-        for zs in range(4):
-            both = jnp.where(sub < 4, out[after, zs].astype(F32), out[before, zs].astype(F32))
-            turned.append(both if zs == 0 else pltpu.roll(both, 32 * zs, 1))
-        out[q, 4] = by_index(which, turned).astype(BF16)
+    def finish(batch):
+        @pl.loop(0, BATCH, unroll=HALO_UNROLL)
+        def _(step):
+            q = batch * BATCH + step
+            after = jnp.minimum(q + 1, parts - 1)
+            before = jnp.maximum(q - 1, 0)
+            both = [
+                jnp.where(sub < 4, kept[after, zs], kept[before, zs]) for zs in range(2 * sections)
+            ]
+            ready[q, 2 * sections] = by_index(which, both).astype(BF16)
+
+        sending(batch).start()
+
+    def sending(batch):
+        strips = pl.ds(batch * BATCH, BATCH)
+        return pltpu.make_async_copy(ready.at[strips], out.at[strips], sent.at[batch])
+
+    batches = parts // BATCH
+
+    @pl.loop(0, batches)
+    def _(batch):
+        @pl.loop(0, BATCH, unroll=MAIN_UNROLL)
+        def _(step):
+            for z in range(sections):
+                for slot in range(2):
+                    one(batch * BATCH + step, z, slot)
+
+        @pl.when(batch > 0)
+        def _():
+            finish(batch - 1)
+
+    finish(batches - 1)
+
+    @pl.loop(0, batches)
+    def _(batch):
+        sending(batch).wait()
 
 
 def assemble_kernel(table, flags, pool, image):
@@ -204,8 +279,9 @@
     row = iota((8, W), 0)
     gain = by_index(row, [bias_one[o] for o in range(8)])
     height = HID_ROWS * 8
-    row = iota((height, W), 0)
-    for p in range(4):
+
+    @pl.loop(0, 4, unroll=UNROLL_ONE)
+    def _(p):
         for b in range(3):
             start = HID_ROWS * b + 6
             stack = jnp.concatenate(
@@ -217,45 +293,47 @@
                 axis=0,
             ).astype(BF16)
             total = jnp.dot(one[...], stack, preferred_element_type=F32)
-            total = jnp.maximum(total.reshape(HID_ROWS, 8, W) + gain, 0.0).reshape(height, W)
+            total = jnp.maximum(total.reshape(HID_ROWS, 8, W) + gain, 0.0)
+            keep = jnp.logical_and(
+                jnp.logical_or(p > 0, flags[2] != 0), jnp.logical_or(p < 3, flags[3] != 0)
+            )
+            layers = [total[r] for r in range(HID_ROWS)]
             if b == 0:
-                total = jnp.where(jnp.logical_or(row >= 8, flags[0] != 0), total, 0.0)
+                layers[0] = jnp.where(flags[0] != 0, layers[0], 0.0)
             if b == 2:
-                total = jnp.where(jnp.logical_or(row < height - 8, flags[1] != 0), total, 0.0)
+                layers[-1] = jnp.where(flags[1] != 0, layers[-1], 0.0)
+            total = jnp.where(keep, jnp.concatenate(layers, axis=0), 0.0)
             hidden[p, height * b : height * b + height, :] = total.astype(BF16)
 
-    @pl.when(flags[2] == 0)
-    def _():
-        hidden[0] = jnp.zeros(hidden.shape[1:], BF16)
-
-    @pl.when(flags[3] == 0)
-    def _():
-        hidden[3] = jnp.zeros(hidden.shape[1:], BF16)
-
     edge = iota((64, W), 1)
-    copies = []
-    for z in range(2):
-        for pair in range(4):
-            halves = []
-            for b in (2 * pair, 2 * pair + 1):
-                stack = jnp.concatenate(
-                    [hidden[z + d, 64 * b : 64 * b + 80, :] for d in range(3)], axis=0
-                )
-                total = jnp.dot(two[...], stack, preferred_element_type=F32)
-                left = jnp.where(edge == 0, 0.0, pltpu.roll(total[0:64], 1, 1))
-                right = jnp.where(edge == W - 1, 0.0, pltpu.roll(total[128:192], W - 1, 1))
-                halves.append(total[64:128] + left + right)
-            rows = pl.ds(16 * pair, 16)
-            for o in range(8):
-                both = jnp.concatenate([half[8 * o : 8 * o + 8] for half in halves], axis=0)
-                stage[o, z, rows, :] = (both + bias_two[o]).astype(BF16)
-            copy = pltpu.make_async_copy(
-                stage.at[:, z, rows, :], out.at[:, z, rows, :], sent.at[4 * z + pair]
-            )
-            copy.start()
-            copies.append(copy)
-    for copy in copies:
-        copy.wait()
+
+    def sending(z, pair):
+        rows = pl.ds(pl.multiple_of(16 * pair, 16), 16)
+        return pltpu.make_async_copy(
+            stage.at[:, z, rows, :], out.at[:, z, rows, :], sent.at[4 * z + pair]
+        )
+
+    @pl.loop(0, 8, unroll=UNROLL_TWO)
+    def _(turn):
+        z = turn >> 2
+        pair = turn & 3
+        halves = []
+        for b in range(2):
+            rows = pl.ds(pl.multiple_of(128 * pair + 64 * b, 64), 80)
+            stack = jnp.concatenate([hidden[z + d, rows, :] for d in range(3)], axis=0)
+            total = jnp.dot(two[...], stack, preferred_element_type=F32)
+            left = jnp.where(edge == 0, 0.0, pltpu.roll(total[0:64], 1, 1))
+            right = jnp.where(edge == W - 1, 0.0, pltpu.roll(total[128:192], W - 1, 1))
+            halves.append(total[64:128] + left + right)
+        rows = pl.ds(pl.multiple_of(16 * pair, 16), 16)
+        for o in range(8):
+            both = jnp.concatenate([half[8 * o : 8 * o + 8] for half in halves], axis=0)
+            stage[o, z, rows, :] = (both + bias_two[o]).astype(BF16)
+        sending(z, pair).start()
+
+    @pl.loop(0, 8)
+    def _(turn):
+        sending(turn >> 2, turn & 3).wait()
 
 
 def smem():
@@ -297,16 +375,25 @@
 
     outgoing = pl.pallas_call(
         render_kernel,
-        out_shape=pltpu.VMEM((parts, 5, 8, 128), BF16),
-        in_specs=[smem()] + [vmem()] * 4 + [pl.BlockSpec(memory_space=pl.ANY)],
-        out_specs=vmem(),
+        out_shape=jax.ShapeDtypeStruct((parts, 5, 8, 128), BF16),
+        in_specs=[pl.BlockSpec(memory_space=pl.ANY)] * 6,
+        out_specs=pl.BlockSpec(memory_space=pl.ANY),
         scratch_shapes=[
+            pltpu.SMEM((parts,), jnp.int32),
+            pltpu.VMEM((sections, 1, parts * 32), jnp.int32),
+            pltpu.VMEM((sections, parts * 32), jnp.int32),
+            pltpu.VMEM((sections, parts * 32), jnp.int32),
+            pltpu.VMEM((sections, parts * 32), jnp.int32),
             pltpu.VMEM((sections, 512, 512), BF16),
             pltpu.VMEM((sections, 4, 512, 128), F32),
+            pltpu.VMEM((parts, 2 * sections, 8, 128), F32),
+            pltpu.VMEM((parts, 5, 8, 128), BF16),
             pltpu.VMEM((8, 128), jnp.int32),
             pltpu.SMEM((8, 128), jnp.int32),
-            pltpu.SemaphoreType.DMA((sections,)),
+            pltpu.SemaphoreType.DMA((5,)),
+            pltpu.SemaphoreType.DMA((2 * sections,)),
             pltpu.SemaphoreType.DMA((1,)),
+            pltpu.SemaphoreType.DMA((parts // BATCH,)),
         ],
         name="render",
     )(

time: 46.2 us -> 43.9 us (0.950)
  Pallas kernels: 13.8 us -> 11.6 us
    pallas_call x1, Pallas kernels: 7.02 us -> 5.04 us  [on_device(): pl.pallas_call(render_kernel, out_shape=jax.ShapeDtypeStruct((parts, 5, 8...]
where the time goes in v4:
time: 43.9 us; the launch traced here: 43.4 us
  starting transfers between devices  13.8 us (31%)
  waiting for transfers between devices  12.4 us (28%)
  Pallas kernels  11.6 us (26%)
  local copies, waits for them, and re-layouts  4.17 us (9%)
  other arithmetic  1.44 us (3%)
    all_to_all x1, starting transfers between devices, on_device(): lax.all_to_all(outgoing, 'xy', split_axis=0, concat_axis=0, tiled=True)  12.6 us
    all_to_all x1, waiting for transfers between devices, on_device(): lax.all_to_all(outgoing, 'xy', split_axis=0, concat_axis=0, tiled=True)  6.44 us
    pallas_call x1, Pallas kernels, on_device(): pl.pallas_call(render_kernel, out_shape=jax.ShapeDtypeStruct((parts, 5, 8...  5.04 us
    pallas_call x1, Pallas kernels, on_device(): pl.pallas_call(conv_kernel, out_shape=jax.ShapeDtypeStruct((8, sections,...  4.03 us
    ppermute x1, waiting for transfers between devices, on_device(): lax.ppermute(image, 'gz', [(i, (i + 1) % depth) for i in range(depth)])  3.12 us
    ppermute x1, waiting for transfers between devices, on_device(): lax.ppermute(image, 'gz', [((i + 1) % depth, i) for i in range(depth)])  2.83 us
    unnamed x9, local copies, waits for them, and re-layouts  2.03 us
    pallas_call x1, Pallas kernels, on_device(): pl.pallas_call(band_kernel, out_shape=(pltpu.VMEM((HID_ROWS * 8, 9 * WIN_...  1.45 us
  transfers between devices with their start and end apart: 3, of which 3 were waited for; matrix products, arithmetic and copies ran while one was open for 8% of the time, Pallas kernels for 3%

profile of v4, /device:TPU:64, one launch (start us, length us, event | category | flops | bytes accessed | tf_op | source)
XLA Modules:
  0.0 43.4 jit_solution(4390564464089646670)
XLA Ops:
  0.0 5.0 %render.1 = bf16[32,5,8,128]{3,2,1,0:T(8,128)(2,1)} custom-call(s32[32]{0:T(128)} %owner_in.1, s32[2,1,1024]{2,1,0:T(1,128)} %bitcast.11, s32[2,1024]{1,0:T(2,128)} %tops_in.1, s32[2,1024]{1,0:T(2,128)} %lefts_in.1, s32[2,1024]{1,0:T(2,128)} %codes_in.1, bf16[2,512,512]{2,1,0:T(8,128)(2,1)} %bitcast.10), custom_call_target="tpu_custom_call" | custom-call | tf_op jit(solution)/shard_map/render/pallas_call | solution.py:376
  5.1 12.6 %all-to-all-start = ((bf16[32,5,8,128]{3,2,1,0:T(8,128)(2,1)}), bf16[32,5,8,128]{3,2,1,0:T(8,128)(2,1)S(1)}, u32[]{:S(2)}, u32[]{:S(2)}) async-start(bf16[32,5,8,128]{3,2,1,0:T(8,128)(2,1)} %render.1), calls=%async_computation | async-start | bytes 655360 | tf_op jit(solution)/shard_map/all_to_all | solution.py:408
  17.6 0.0 copy-start.1
  17.7 0.7 %copy-done.1 = s32[2,1024,1]{1,2,0:T(1,128)S(1)} copy-done((s32[2,1024,1]{1,2,0:T(1,128)S(1)}, s32[2,1024,1]{1,2,0:T(1,128)}, u32[]{:S(2)}) %copy-start.1) | copy-done | bytes 8216
  18.4 0.0 copy-start.2
  18.4 0.1 iota_compare_fusion.2
  18.5 0.6 %copy-done.2 = bf16[8,1,3,3,3]{0,4,3,2,1:T(4,128)(2,1)S(1)} copy-done((bf16[8,1,3,3,3]{0,4,3,2,1:T(4,128)(2,1)S(1)}, bf16[8,1,3,3,3]{0,4,3,2,1:T(4,128)(2,1)}, u32[]{:S(2)}) %copy-start.2) | copy-done | bytes 456
  19.1 0.7 %copy.17.flat_one = bf16[8,27]{1,0:T(8,128)(2,1)} copy(bf16[8,27]{0,1:T(8,128)(2,1)S(1)} %reshape.68) | data formatting | bytes 864 | tf_op jit(solution)/shard_map/reshape | solution.py:436
  19.8 0.0 copy-start
  19.8 0.1 broadcast_in_dim.38
  19.9 0.1 select_reduce_fusion.1
  20.0 0.0 copy-start.3
  20.0 0.6 %copy-done.3 = s32[32]{0:T(128)S(1)} copy-done((s32[32]{0:T(128)S(1)}, s32[32]{0:T(128)}, u32[]{:S(2)}) %copy-start.3) | copy-done | bytes 152
  20.6 0.3 select_reduce_fusion
  20.9 0.3 and_reduce_fusion
  21.2 0.7 %add.28.table = s32[192]{0:T(256)} reshape(s32[2,3,32]{2,1,0:T(4,128)S(1)} %convert_add_fusion) | data formatting | bytes 1536 | tf_op jit(solution)/shard_map/add | solution.py:424
  21.8 0.0 copy-done
  21.8 0.1 copy.16
  22.0 0.7 %copy.18.flat_two = bf16[8,216]{1,0:T(8,128)(2,1)} copy(bf16[8,216]{0,1:T(8,128)(2,1)S(1)} %reshape.69) | data formatting | bytes 6912 | tf_op jit(solution)/shard_map/reshape | solution.py:436
  22.7 1.5 %bands.1 = (bf16[176,216]{1,0:T(8,128)(2,1)S(1)}, bf16[192,240]{1,0:T(8,128)(2,1)S(1)}) custom-call(bf16[8,27]{1,0:T(8,128)(2,1)} %copy.17.flat_one, bf16[8,216]{1,0:T(8,128)(2,1)} %copy.18.flat_two), custom_call_target="tpu_custom_call" | custom-call | tf_op jit(solution)/shard_map/bands/pallas_call | solution.py:427
  24.1 0.7 %add_convert_fusion.flags = s32[4]{0:T(128)} fusion(pred[1]{0:T(512)(128)(4,1)} %bitcast.5, pred[1]{0:T(512)(128)(4,1)} %bitcast.4, pred[1]{0:T(512)(128)(4,1)} %bitcast.3, pred[1]{0:T(512)(128)(4,1)} %bitcast.2), kind=kLoop, calls=%fused_computation.7 | loop fusion | flops 16 | bytes 20 | tf_op jit(solution)/shard_map/convert_element_type | solution.py:425
  24.8 6.4 %all-to-all-done.pool = bf16[32,5,8,128]{3,2,1,0:T(8,128)(2,1)S(1)} async-done(((bf16[32,5,8,128]{3,2,1,0:T(8,128)(2,1)}), bf16[32,5,8,128]{3,2,1,0:T(8,128)(2,1)S(1)}, u32[]{:S(2)}, u32[]{:S(2)}) %all-to-all-start) | async-done | bytes 327712 | tf_op jit(solution)/shard_map/all_to_all | solution.py:408
  31.2 1.0 %assemble.1.own = bf16[2,80,512]{2,1,0:T(8,128)(2,1)S(1)} custom-call(s32[192]{0:T(256)} %add.28.table, s32[4]{0:T(128)} %add_convert_fusion.flags, bf16[32,5,8,128]{3,2,1,0:T(8,128)(2,1)S(1)} %all-to-all-done.pool), custom_call_target="tpu_custom_call" | custom-call | tf_op jit(solution)/shard_map/assemble/pallas_call | solution.py:441
  32.3 1.2 %collective-permute-start.1 = (bf16[2,80,512]{2,1,0:T(8,128)(2,1)S(1)}, bf16[2,80,512]{2,1,0:T(8,128)(2,1)S(1)}, u32[]{:S(2)}, u32[]{:S(2)}) collective-permute-start(bf16[2,80,512]{2,1,0:T(8,128)(2,1)S(1)} %assemble.1.own), channel_id=1, source_target_pairs={{1,0},{2,1},{3,2},{4,3},{5,4},{6,5},{7,6},{8,7},{9,8},{10,9},{11,1... | collective-permute-start | bytes 491528 | tf_op jit(solution)/shard_map/ppermute | solution.py:450
  33.5 0.0 collective-permute-start
  33.5 2.8 %collective-permute-done.1.after = bf16[2,80,512]{2,1,0:T(8,128)(2,1)S(1)} collective-permute-done((bf16[2,80,512]{2,1,0:T(8,128)(2,1)S(1)}, bf16[2,80,512]{2,1,0:T(8,128)(2,1)S(1)}, u32[]{:S(2)}, u32[]{:S(2)}) %collective-permute-start.1) | collective-permute-done | bytes 163872 | tf_op jit(solution)/shard_map/ppermute | solution.py:450
  36.3 3.1 %collective-permute-done.before = bf16[2,80,512]{2,1,0:T(8,128)(2,1)S(1)} collective-permute-done((bf16[2,80,512]{2,1,0:T(8,128)(2,1)S(1)}, bf16[2,80,512]{2,1,0:T(8,128)(2,1)S(1)}, u32[]{:S(2)}, u32[]{:S(2)}) %collective-permute-start) | collective-permute-done | bytes 163872 | tf_op jit(solution)/shard_map/ppermute | solution.py:449
  39.4 4.0 %convolve.1 = bf16[8,2,64,512]{3,2,1,0:T(8,128)(2,1)} custom-call(s32[4]{0:T(128)} %add_convert_fusion.flags, f32[8]{0:T(128)} %bias_one.1, f32[8]{0:T(128)} %bias_two.1, bf16[2,80,512]{2,1,0:T(8,128)(2,1)S(1)} %collective-permute-done.before, bf16[2,80,512]{2,1,0:T(8,128)(2,1)S(1)} %assemble.1.own, bf16[2,80,512]{2,1,0:T(8,128)(2,1)S(1)} %collective-permute-done.1.after, ...), custom_call_target="tpu_custom_call" | custom-call | tf_op jit(solution)/shard_map/convolve/pallas_call | solution.py:452
  (6 shorter events, 0.1 us)
Async XLA Ops:
  5.1 26.2 %all-to-all-start = ((bf16[32,5,8,128]{3,2,1,0:T(8,128)(2,1)}), bf16[32,5,8,128]{3,2,1,0:T(8,128)(2,1)S(1)}, u32[]{:S(2)}, u32[]{:S(2)}) async-start(bf16[32,5,8,128]{3,2,1,0:T(8,128)(2,1)} %render.1), calls=%async_computation | async-start | bytes 655360 | tf_op jit(solution)/shard_map/all_to_all | solution.py:408
  17.6 0.7 %copy-start.1 = (s32[2,1024,1]{1,2,0:T(1,128)S(1)}, s32[2,1024,1]{1,2,0:T(1,128)}, u32[]{:S(2)}) copy-start(s32[2,1024,1]{1,2,0:T(1,128)} %param.11) | copy-start | bytes 24580
  18.4 0.7 %copy-start.2 = (bf16[8,1,3,3,3]{0,4,3,2,1:T(4,128)(2,1)S(1)}, bf16[8,1,3,3,3]{0,4,3,2,1:T(4,128)(2,1)}, u32[]{:S(2)}) copy-start(bf16[8,1,3,3,3]{0,4,3,2,1:T(4,128)(2,1)} %param.16) | copy-start | bytes 1300
  19.8 2.0 %copy-start = (bf16[8,8,3,3,3]{1,0,4,3,2:T(8,128)(2,1)S(1)}, bf16[8,8,3,3,3]{1,0,4,3,2:T(8,128)(2,1)}, u32[]{:S(2)}) copy-start(bf16[8,8,3,3,3]{1,0,4,3,2:T(8,128)(2,1)} %param.18) | copy-start | bytes 10372
  20.0 0.7 %copy-start.3 = (s32[32]{0:T(128)S(1)}, s32[32]{0:T(128)}, u32[]{:S(2)}) copy-start(s32[32]{0:T(128)} %owner_in.1) | copy-start | bytes 388
  32.3 4.0 %collective-permute-start.1 = (bf16[2,80,512]{2,1,0:T(8,128)(2,1)S(1)}, bf16[2,80,512]{2,1,0:T(8,128)(2,1)S(1)}, u32[]{:S(2)}, u32[]{:S(2)}) collective-permute-start(bf16[2,80,512]{2,1,0:T(8,128)(2,1)S(1)} %assemble.1.own), channel_id=1, source_target_pairs={{1,0},{2,1},{3,2},{4,3},{5,4},{6,5},{7,6},{8,7},{9,8},{10,9},{11,1... | collective-permute-start | bytes 491528 | tf_op jit(solution)/shard_map/ppermute | solution.py:450
  33.5 6.0 %collective-permute-start = (bf16[2,80,512]{2,1,0:T(8,128)(2,1)S(1)}, bf16[2,80,512]{2,1,0:T(8,128)(2,1)S(1)}, u32[]{:S(2)}, u32[]{:S(2)}) collective-permute-start(bf16[2,80,512]{2,1,0:T(8,128)(2,1)S(1)} %assemble.1.own), channel_id=1, source_target_pairs={{0,1},{1,2},{2,3},{3,4},{4,5},{5,6},{6,7},{7,8},{8,9},{9,10},{10,1... | collective-permute-start | bytes 491528 | tf_op jit(solution)/shard_map/ppermute | solution.py:449

commit v5 on v4

--- a/solution.py
+++ b/solution.py
@@ -9,7 +9,7 @@
 W = 512
 HID_ROWS = 22
 WIN_ROWS = 24
-IMG_ROWS = 80
+IMG_ROWS = 72
 BATCH = 8
 MAIN_UNROLL = 8
 HALO_UNROLL = 4
@@ -90,10 +90,12 @@
     count = source.shape[2]
     blank = jnp.full((8 - sections, count), -1, jnp.int32)
     match = jnp.concatenate([source[z] for z in range(sections)] + [blank], axis=0) == mine
-    within = iota((8, count), 1) & 31
-    rank = match.astype(jnp.int32)
-    for reach in (1, 2, 4, 8, 16):
-        rank = rank + jnp.where(within >= reach, pltpu.roll(rank, reach, 1), 0)
+    marks = match.astype(F32)
+    tall = jnp.concatenate([marks[:, t : t + 128] for t in range(0, count, 128)], axis=0)
+    early, late = iota((128, 128), 0), iota((128, 128), 1)
+    upto = jnp.logical_and(early // 32 == late // 32, early <= late).astype(F32)
+    ranks = jnp.dot(tall.astype(BF16), upto.astype(BF16), preferred_element_type=F32)
+    rank = jnp.concatenate([ranks[t : t + 8] for t in range(0, count // 16, 8)], axis=1)
     packed = tops[...] + (lefts[...] << 9) + (codes[...] << 18)
     packed = jnp.concatenate([packed, blank], axis=0)
     pieces = []
@@ -197,7 +199,9 @@
         sending(batch).wait()
 
 
-def assemble_kernel(table, flags, pool, image):
+def assemble_kernel(table, pool, image):
+    me = lax.axis_index("xy")
+    bottom = lax.axis_size("xy") - 1
     lane = iota((8, 128), 1)
     group = lane // 32
     sections = image.shape[0]
@@ -217,7 +221,7 @@
                 k, zs = entry(z, 2, 4 * c + v)
                 piece = pool[k, 4].astype(F32)
                 feet.append(pltpu.roll(piece, (32 * (v - zs) + 256) & 127, 1))
-            rows.append(jnp.where(flags[0] == 0, 0.0, by_index(group, heads)))
+            rows.append(jnp.where(me == 0, 0.0, by_index(group, heads)))
             for u in range(2):
                 blocks = []
                 for v in range(4):
@@ -229,11 +233,16 @@
                         for v in range(4)
                     ]
                     rows.append(by_index(group, turned))
-            rows.append(jnp.where(flags[1] == 0, 0.0, by_index(group, feet)))
-            image[z, :, 128 * c : 128 * c + 128] = jnp.concatenate(rows, axis=0).astype(BF16)
-
-
-def band_kernel(flat_one, flat_two, one, two):
+            rows.append(jnp.where(me == bottom, 0.0, by_index(group, feet)))
+            strip = jnp.concatenate(rows, axis=0)[4:76]
+            image[z, :, 128 * c : 128 * c + 128] = strip.astype(BF16)
+
+
+def band_kernel(bias_one, bias_two, flat_one, flat_two, one, two, gain, lift):
+    row = iota(gain.shape, 0)
+    gain[...] = by_index(row, [bias_one[o] for o in range(8)])
+    row = iota(lift.shape, 0) // 8
+    lift[...] = by_index(row, [bias_two[o] for o in range(8)])
     rows, cols = one.shape
     col = iota((27, cols), 1)
     base = (col // WIN_ROWS) % 3 * 9 + col // (3 * WIN_ROWS)
@@ -262,28 +271,30 @@
 
 
 def conv_kernel(
-    flags, bias_one, bias_two, before, own, after, one, two, out, shifted, hidden, stage, sent
+    gain_in, lift_in, before, own, after, one, two, out, shifted, hidden, stage, sent
 ):
+    me, deep = lax.axis_index("xy"), lax.axis_index("gz")
+    bottom, last = lax.axis_size("xy") - 1, lax.axis_size("gz") - 1
     lane = iota((IMG_ROWS, W), 1)
     for number, (ref, z) in enumerate(
         [(before, 0), (before, 1), (own, 0), (own, 1), (after, 0), (after, 1)]
     ):
         plane = ref[z].astype(F32)
         if number < 2:
-            plane = jnp.where(flags[2] == 0, 0.0, plane)
+            plane = jnp.where(deep == 0, 0.0, plane)
         if number >= 4:
-            plane = jnp.where(flags[3] == 0, 0.0, plane)
+            plane = jnp.where(deep == last, 0.0, plane)
         shifted[number, 0] = jnp.where(lane == 0, 0.0, pltpu.roll(plane, 1, 1))
         shifted[number, 1] = plane
         shifted[number, 2] = jnp.where(lane == W - 1, 0.0, pltpu.roll(plane, W - 1, 1))
-    row = iota((8, W), 0)
-    gain = by_index(row, [bias_one[o] for o in range(8)])
+    gain = jnp.concatenate([gain_in[...]] * 4, axis=1)
+    lift = jnp.concatenate([lift_in[...]] * 4, axis=1)
     height = HID_ROWS * 8
 
     @pl.loop(0, 4, unroll=UNROLL_ONE)
     def _(p):
         for b in range(3):
-            start = HID_ROWS * b + 6
+            start = HID_ROWS * b + 2
             stack = jnp.concatenate(
                 [
                     shifted[p + d, f, start : start + WIN_ROWS, :]
@@ -295,13 +306,13 @@
             total = jnp.dot(one[...], stack, preferred_element_type=F32)
             total = jnp.maximum(total.reshape(HID_ROWS, 8, W) + gain, 0.0)
             keep = jnp.logical_and(
-                jnp.logical_or(p > 0, flags[2] != 0), jnp.logical_or(p < 3, flags[3] != 0)
+                jnp.logical_or(p > 0, deep > 0), jnp.logical_or(p < 3, deep < last)
             )
             layers = [total[r] for r in range(HID_ROWS)]
             if b == 0:
-                layers[0] = jnp.where(flags[0] != 0, layers[0], 0.0)
+                layers[0] = jnp.where(me > 0, layers[0], 0.0)
             if b == 2:
-                layers[-1] = jnp.where(flags[1] != 0, layers[-1], 0.0)
+                layers[-1] = jnp.where(me < bottom, layers[-1], 0.0)
             total = jnp.where(keep, jnp.concatenate(layers, axis=0), 0.0)
             hidden[p, height * b : height * b + height, :] = total.astype(BF16)
 
@@ -324,11 +335,11 @@
             total = jnp.dot(two[...], stack, preferred_element_type=F32)
             left = jnp.where(edge == 0, 0.0, pltpu.roll(total[0:64], 1, 1))
             right = jnp.where(edge == W - 1, 0.0, pltpu.roll(total[128:192], W - 1, 1))
-            halves.append(total[64:128] + left + right)
+            halves.append(total[64:128] + left + right + lift)
         rows = pl.ds(pl.multiple_of(16 * pair, 16), 16)
         for o in range(8):
             both = jnp.concatenate([half[8 * o : 8 * o + 8] for half in halves], axis=0)
-            stage[o, z, rows, :] = (both + bias_two[o]).astype(BF16)
+            stage[o, z, rows, :] = both.astype(BF16)
         sending(z, pair).start()
 
     @pl.loop(0, 8)
@@ -422,29 +433,30 @@
         axis=-1,
     )
     places = (holder * 2 + second.astype(jnp.int32)).reshape(-1)
-    flags = jnp.stack([me > 0, me < parts - 1, deep > 0, deep < depth - 1]).astype(jnp.int32)
-
-    banded_one, banded_two = pl.pallas_call(
+
+    banded_one, banded_two, gain, lift = pl.pallas_call(
         band_kernel,
         out_shape=(
             pltpu.VMEM((HID_ROWS * 8, 9 * WIN_ROWS), BF16),
             pltpu.VMEM((192, 240), BF16),
+            pltpu.VMEM((8, 128), F32),
+            pltpu.VMEM((64, 128), F32),
         ),
-        in_specs=[vmem(), vmem()],
-        out_specs=(vmem(), vmem()),
+        in_specs=[smem(), smem(), vmem(), vmem()],
+        out_specs=(vmem(),) * 4,
         name="bands",
-    )(weight_one.reshape(8, 27), weight_two.reshape(8, 216))
-
-    received, places, flags, banded_one, banded_two = lax.optimization_barrier(
-        (received, places, flags, banded_one, banded_two)
+    )(bias_one, bias_two, weight_one.reshape(8, 27), weight_two.reshape(8, 216))
+
+    received, places, banded_one, banded_two, gain, lift = lax.optimization_barrier(
+        (received, places, banded_one, banded_two, gain, lift)
     )
     image = pl.pallas_call(
         assemble_kernel,
         out_shape=pltpu.VMEM((sections, IMG_ROWS, W), BF16),
-        in_specs=[smem(), smem(), vmem()],
+        in_specs=[smem(), vmem()],
         out_specs=vmem(),
         name="assemble",
-    )(in_smem(places), in_smem(flags), in_vmem(received))
+    )(in_smem(places), in_vmem(received))
 
     before = lax.ppermute(image, "gz", [(i, (i + 1) % depth) for i in range(depth)])
     after = lax.ppermute(image, "gz", [((i + 1) % depth, i) for i in range(depth)])
@@ -452,7 +464,7 @@
     return pl.pallas_call(
         conv_kernel,
         out_shape=jax.ShapeDtypeStruct((8, sections, 64, W), BF16),
-        in_specs=[smem()] * 3 + [vmem()] * 5,
+        in_specs=[vmem()] * 7,
         out_specs=pl.BlockSpec(memory_space=pl.ANY),
         scratch_shapes=[
             pltpu.VMEM((6, 3, IMG_ROWS, W), F32),
@@ -462,9 +474,8 @@
         ],
         name="convolve",
     )(
-        in_smem(flags),
-        bias_one,
-        bias_two,
+        in_vmem(gain),
+        in_vmem(lift),
         in_vmem(before),
         in_vmem(image),
         in_vmem(after),

time: 43.9 us -> 42.6 us (0.970)
  waiting for transfers between devices: 12.4 us -> 13.6 us
  Pallas kernels: 11.6 us -> 10.5 us
  local copies, waits for them, and re-layouts: 4.17 us -> 3.44 us
  other arithmetic: 1.44 us -> 0.76 us
    all_to_all x1, waiting for transfers between devices: 6.44 us -> 7.85 us  [on_device(): lax.all_to_all(outgoing, 'xy', split_axis=0, concat_axis=0, tiled=True)]
    pallas_call x1, Pallas kernels: 4.03 us -> 3.17 us  [on_device(): pl.pallas_call(conv_kernel, out_shape=jax.ShapeDtypeStruct((8, sections,...]
    unnamed x9, local copies, waits for them, and re-layouts: 2.03 us -> 1.3 us
    convert_element_type x1 -> x0, other arithmetic: 0.67 us -> none  [on_device(): jnp.stack([me > 0, me < parts - 1, deep > 0, deep < depth - 1])]
  transfers between devices with their start and end apart: 3 -> 3, of which waited for: 3 -> 3; matrix products, arithmetic and copies ran while one was open for 8% -> 7% of each run, Pallas kernels for 3% -> 3%
where the time goes in v5:
time: 42.6 us; the launch traced here: 42.2 us
  starting transfers between devices  13.8 us (32%)
  waiting for transfers between devices  13.6 us (32%)
  Pallas kernels  10.5 us (25%)
  local copies, waits for them, and re-layouts  3.44 us (8%)
  other arithmetic  0.76 us (2%)
    all_to_all x1, starting transfers between devices, on_device(): lax.all_to_all(outgoing, 'xy', split_axis=0, concat_axis=0, tiled=True)  12.6 us
    all_to_all x1, waiting for transfers between devices, on_device(): lax.all_to_all(outgoing, 'xy', split_axis=0, concat_axis=0, tiled=True)  7.85 us
    pallas_call x1, Pallas kernels, on_device(): pl.pallas_call(render_kernel, out_shape=jax.ShapeDtypeStruct((parts, 5, 8...  4.8 us
    pallas_call x1, Pallas kernels, on_device(): pl.pallas_call(conv_kernel, out_shape=jax.ShapeDtypeStruct((8, sections,...  3.17 us
    ppermute x1, waiting for transfers between devices, on_device(): lax.ppermute(image, 'gz', [(i, (i + 1) % depth) for i in range(depth)])  3.1 us
    ppermute x1, waiting for transfers between devices, on_device(): lax.ppermute(image, 'gz', [((i + 1) % depth, i) for i in range(depth)])  2.67 us
    pallas_call x1, Pallas kernels, on_device(): pl.pallas_call(band_kernel, out_shape=(pltpu.VMEM((HID_ROWS * 8, 9 * WIN_...  1.46 us
    unnamed x9, local copies, waits for them, and re-layouts  1.3 us
  transfers between devices with their start and end apart: 3, of which 3 were waited for; matrix products, arithmetic and copies ran while one was open for 7% of the time, Pallas kernels for 3%

profile of v5, /device:TPU:64, one launch (start us, length us, event | category | flops | bytes accessed | tf_op | source)
XLA Modules:
  0.0 42.2 jit_solution(18278087614818458456)
XLA Ops:
  0.0 4.8 %render.1 = bf16[32,5,8,128]{3,2,1,0:T(8,128)(2,1)} custom-call(s32[32]{0:T(128)} %owner_in.1, s32[2,1,1024]{2,1,0:T(1,128)} %bitcast.7, s32[2,1024]{1,0:T(2,128)} %tops_in.1, s32[2,1024]{1,0:T(2,128)} %lefts_in.1, s32[2,1024]{1,0:T(2,128)} %codes_in.1, bf16[2,512,512]{2,1,0:T(8,128)(2,1)} %bitcast.6), custom_call_target="tpu_custom_call" | custom-call | tf_op jit(solution)/shard_map/render/pallas_call | solution.py:387
  4.8 12.6 %all-to-all-start = ((bf16[32,5,8,128]{3,2,1,0:T(8,128)(2,1)}), bf16[32,5,8,128]{3,2,1,0:T(8,128)(2,1)S(1)}, u32[]{:S(2)}, u32[]{:S(2)}) async-start(bf16[32,5,8,128]{3,2,1,0:T(8,128)(2,1)} %render.1), calls=%async_computation | async-start | bytes 655360 | tf_op jit(solution)/shard_map/all_to_all | solution.py:419
  17.4 0.0 copy-start.2
  17.4 0.1 iota_compare_fusion.2
  17.5 0.6 %copy-done.2 = bf16[8,1,3,3,3]{0,4,3,2,1:T(4,128)(2,1)S(1)} copy-done((bf16[8,1,3,3,3]{0,4,3,2,1:T(4,128)(2,1)S(1)}, bf16[8,1,3,3,3]{0,4,3,2,1:T(4,128)(2,1)}, u32[]{:S(2)}) %copy-start.2) | copy-done | bytes 456
  18.1 0.0 copy-start.1
  18.1 0.7 %copy.17.flat_one = bf16[8,27]{1,0:T(8,128)(2,1)} copy(bf16[8,27]{0,1:T(8,128)(2,1)S(1)} %reshape.68) | data formatting | bytes 864 | tf_op jit(solution)/shard_map/reshape | solution.py:448
  18.8 0.0 copy-done.1
  18.9 0.0 copy-start
  18.9 0.1 broadcast_in_dim.38
  19.0 0.0 copy-start.3
  19.0 0.1 select_reduce_fusion.1
  19.1 0.6 %copy-done.3 = s32[32]{0:T(128)S(1)} copy-done((s32[32]{0:T(128)S(1)}, s32[32]{0:T(128)}, u32[]{:S(2)}) %copy-start.3) | copy-done | bytes 152
  19.6 0.3 select_reduce_fusion
  19.9 0.3 and_reduce_fusion
  20.2 0.7 %add.28.table = s32[192]{0:T(256)} reshape(s32[2,3,32]{2,1,0:T(4,128)S(1)} %convert_add_fusion) | data formatting | bytes 1536 | tf_op jit(solution)/shard_map/add | solution.py:435
  20.8 0.0 copy-done
  20.8 0.1 copy.16
  21.0 0.7 %copy.18.flat_two = bf16[8,216]{1,0:T(8,128)(2,1)} copy(bf16[8,216]{0,1:T(8,128)(2,1)S(1)} %reshape.69) | data formatting | bytes 6912 | tf_op jit(solution)/shard_map/reshape | solution.py:448
  21.7 1.5 %bands.1 = (bf16[176,216]{1,0:T(8,128)(2,1)S(1)}, bf16[192,240]{1,0:T(8,128)(2,1)S(1)}, f32[8,128]{1,0:T(8,128)S(1)}, f32[64,128]{1,0:T(8,128)S(1)}) custom-call(f32[8]{0:T(128)} %bias_one.1, f32[8]{0:T(128)} %bias_two.1, bf16[8,27]{1,0:T(8,128)(2,1)} %copy.17.flat_one, bf16[8,216]{1,0:T(8,128)(2,1)} %copy.18.flat_two), custom_call_target="tpu_custom_call" | custom-call | tf_op jit(solution)/shard_map/bands/pallas_call | solution.py:437
  23.1 7.9 %all-to-all-done.pool = bf16[32,5,8,128]{3,2,1,0:T(8,128)(2,1)S(1)} async-done(((bf16[32,5,8,128]{3,2,1,0:T(8,128)(2,1)}), bf16[32,5,8,128]{3,2,1,0:T(8,128)(2,1)S(1)}, u32[]{:S(2)}, u32[]{:S(2)}) %all-to-all-start) | async-done | bytes 327712 | tf_op jit(solution)/shard_map/all_to_all | solution.py:419
  31.0 1.0 %assemble.1.own = bf16[2,72,512]{2,1,0:T(8,128)(2,1)S(1)} custom-call(s32[192]{0:T(256)} %add.28.table, bf16[32,5,8,128]{3,2,1,0:T(8,128)(2,1)S(1)} %all-to-all-done.pool), custom_call_target="tpu_custom_call" | custom-call | tf_op jit(solution)/shard_map/assemble/pallas_call | solution.py:453
  32.0 1.2 %collective-permute-start.1 = (bf16[2,72,512]{2,1,0:T(8,128)(2,1)S(1)}, bf16[2,72,512]{2,1,0:T(8,128)(2,1)S(1)}, u32[]{:S(2)}, u32[]{:S(2)}) collective-permute-start(bf16[2,72,512]{2,1,0:T(8,128)(2,1)S(1)} %assemble.1.own), channel_id=1, source_target_pairs={{1,0},{2,1},{3,2},{4,3},{5,4},{6,5},{7,6},{8,7},{9,8},{10,9},{11,1... | collective-permute-start | bytes 442376 | tf_op jit(solution)/shard_map/ppermute | solution.py:462
  33.2 0.0 collective-permute-start
  33.2 2.7 %collective-permute-done.1.after = bf16[2,72,512]{2,1,0:T(8,128)(2,1)S(1)} collective-permute-done((bf16[2,72,512]{2,1,0:T(8,128)(2,1)S(1)}, bf16[2,72,512]{2,1,0:T(8,128)(2,1)S(1)}, u32[]{:S(2)}, u32[]{:S(2)}) %collective-permute-start.1) | collective-permute-done | bytes 147488 | tf_op jit(solution)/shard_map/ppermute | solution.py:462
  35.9 3.1 %collective-permute-done.before = bf16[2,72,512]{2,1,0:T(8,128)(2,1)S(1)} collective-permute-done((bf16[2,72,512]{2,1,0:T(8,128)(2,1)S(1)}, bf16[2,72,512]{2,1,0:T(8,128)(2,1)S(1)}, u32[]{:S(2)}, u32[]{:S(2)}) %collective-permute-start) | collective-permute-done | bytes 147488 | tf_op jit(solution)/shard_map/ppermute | solution.py:461
  39.0 3.2 %convolve.1 = bf16[8,2,64,512]{3,2,1,0:T(8,128)(2,1)} custom-call(f32[8,128]{1,0:T(8,128)S(1)} %get-tuple-element.19.gain_in, f32[64,128]{1,0:T(8,128)S(1)} %get-tuple-element.20.lift_in, bf16[2,72,512]{2,1,0:T(8,128)(2,1)S(1)} %collective-permute-done.before, bf16[2,72,512]{2,1,0:T(8,128)(2,1)S(1)} %assemble.1.own, ...), custom_call_target="tpu_custom_call" | custom-call | tf_op jit(solution)/shard_map/convolve/pallas_call | solution.py:464
  (6 shorter events, 0.1 us)
Async XLA Ops:
  4.8 26.2 %all-to-all-start = ((bf16[32,5,8,128]{3,2,1,0:T(8,128)(2,1)}), bf16[32,5,8,128]{3,2,1,0:T(8,128)(2,1)S(1)}, u32[]{:S(2)}, u32[]{:S(2)}) async-start(bf16[32,5,8,128]{3,2,1,0:T(8,128)(2,1)} %render.1), calls=%async_computation | async-start | bytes 655360 | tf_op jit(solution)/shard_map/all_to_all | solution.py:419
  17.4 0.7 %copy-start.2 = (bf16[8,1,3,3,3]{0,4,3,2,1:T(4,128)(2,1)S(1)}, bf16[8,1,3,3,3]{0,4,3,2,1:T(4,128)(2,1)}, u32[]{:S(2)}) copy-start(bf16[8,1,3,3,3]{0,4,3,2,1:T(4,128)(2,1)} %param.16) | copy-start | bytes 1300
  18.1 0.7 %copy-start.1 = (s32[2,1024,1]{1,2,0:T(1,128)S(1)}, s32[2,1024,1]{1,2,0:T(1,128)}, u32[]{:S(2)}) copy-start(s32[2,1024,1]{1,2,0:T(1,128)} %param.11) | copy-start | bytes 24580
  18.9 2.0 %copy-start = (bf16[8,8,3,3,3]{1,0,4,3,2:T(8,128)(2,1)S(1)}, bf16[8,8,3,3,3]{1,0,4,3,2:T(8,128)(2,1)}, u32[]{:S(2)}) copy-start(bf16[8,8,3,3,3]{1,0,4,3,2:T(8,128)(2,1)} %param.18) | copy-start | bytes 10372
  19.0 0.7 %copy-start.3 = (s32[32]{0:T(128)S(1)}, s32[32]{0:T(128)}, u32[]{:S(2)}) copy-start(s32[32]{0:T(128)} %owner_in.1) | copy-start | bytes 388
  32.0 3.9 %collective-permute-start.1 = (bf16[2,72,512]{2,1,0:T(8,128)(2,1)S(1)}, bf16[2,72,512]{2,1,0:T(8,128)(2,1)S(1)}, u32[]{:S(2)}, u32[]{:S(2)}) collective-permute-start(bf16[2,72,512]{2,1,0:T(8,128)(2,1)S(1)} %assemble.1.own), channel_id=1, source_target_pairs={{1,0},{2,1},{3,2},{4,3},{5,4},{6,5},{7,6},{8,7},{9,8},{10,9},{11,1... | collective-permute-start | bytes 442376 | tf_op jit(solution)/shard_map/ppermute | solution.py:462
  33.2 5.8 %collective-permute-start = (bf16[2,72,512]{2,1,0:T(8,128)(2,1)S(1)}, bf16[2,72,512]{2,1,0:T(8,128)(2,1)S(1)}, u32[]{:S(2)}, u32[]{:S(2)}) collective-permute-start(bf16[2,72,512]{2,1,0:T(8,128)(2,1)S(1)} %assemble.1.own), channel_id=1, source_target_pairs={{0,1},{1,2},{2,3},{3,4},{4,5},{5,6},{6,7},{7,8},{8,9},{9,10},{10,1... | collective-permute-start | bytes 442376 | tf_op jit(solution)/shard_map/ppermute | solution.py:461

commit v6 on v5

--- a/solution.py
+++ b/solution.py
@@ -13,7 +13,6 @@
 BATCH = 8
 MAIN_UNROLL = 8
 HALO_UNROLL = 4
-UNROLL_ONE = 4
 UNROLL_TWO = 8
 F32 = jnp.float32
 BF16 = jnp.bfloat16
@@ -28,6 +27,20 @@
     for number in range(len(choices) - 2, -1, -1):
         result = jnp.where(which == number, choices[number], result)
     return result
+
+
+def step_right(block):
+    first = iota((block.shape[0], 128), 1) == 0
+    turned = [pltpu.roll(block[:, c : c + 128], 1, 1) for c in range(0, W, 128)]
+    before = [0.0] + turned[:-1]
+    return jnp.concatenate([jnp.where(first, x, y) for x, y in zip(before, turned)], axis=1)
+
+
+def step_left(block):
+    final = iota((block.shape[0], 128), 1) == 127
+    turned = [pltpu.roll(block[:, c : c + 128], 127, 1) for c in range(0, W, 128)]
+    after = turned[1:] + [0.0]
+    return jnp.concatenate([jnp.where(final, x, y) for x, y in zip(after, turned)], axis=1)
 
 
 def render_kernel(
@@ -80,22 +93,25 @@
     ]
     for copy in small + copies:
         copy.start()
-    for copy in small:
+    count = source.shape[2]
+    early, late = iota((128, 128), 0), iota((128, 128), 1)
+    upto = jnp.logical_and(early // 32 == late // 32, early <= late).astype(F32).astype(BF16)
+    strips = (iota((count, 128), 0) // 32 == iota((count, 128), 1)).astype(F32).astype(BF16)
+    for copy in small[:2]:
         copy.wait()
 
     me = lax.axis_index("xy")
     mine = jnp.int32(0)
     for k in range(parts):
         mine = jnp.where(owner[k] == me, k, mine)
-    count = source.shape[2]
     blank = jnp.full((8 - sections, count), -1, jnp.int32)
     match = jnp.concatenate([source[z] for z in range(sections)] + [blank], axis=0) == mine
     marks = match.astype(F32)
     tall = jnp.concatenate([marks[:, t : t + 128] for t in range(0, count, 128)], axis=0)
-    early, late = iota((128, 128), 0), iota((128, 128), 1)
-    upto = jnp.logical_and(early // 32 == late // 32, early <= late).astype(F32)
-    ranks = jnp.dot(tall.astype(BF16), upto.astype(BF16), preferred_element_type=F32)
+    ranks = jnp.dot(tall.astype(BF16), upto, preferred_element_type=F32)
     rank = jnp.concatenate([ranks[t : t + 8] for t in range(0, count // 16, 8)], axis=1)
+    for copy in small[2:]:
+        copy.wait()
     packed = tops[...] + (lefts[...] << 9) + (codes[...] << 18)
     packed = jnp.concatenate([packed, blank], axis=0)
     pieces = []
@@ -103,7 +119,6 @@
         chosen = jnp.where(jnp.logical_and(match, rank == slot + 1), packed, 0)
         for k in range(3):
             pieces.append(((chosen >> (8 * k)) & 255).astype(F32))
-    strips = (iota((count, 128), 0) // 32 == iota((count, 128), 1)).astype(F32).astype(BF16)
     sums = jnp.dot(
         jnp.concatenate(pieces, axis=0).astype(BF16), strips, preferred_element_type=F32
     ).astype(jnp.int32)
@@ -149,14 +164,15 @@
                 wide[z, near, pl.ds(y + (8 * g + 1), 8), :],
             )
             mixed = (1.0 - a) * upper + a * lower
-            here.append(pltpu.roll(mixed, (32 * g + 128 - low) & 127, 1))
-        left = by_index(group, here)
-        spill = by_index(group, here[3:] + here[:3])
-        right = pltpu.roll(jnp.where(starts, spill, left), 127, 1)
+            here.append(mixed if g == 0 else pltpu.roll(mixed, 32 * g, 1))
+        turn = (lane - low) & 127
+        left = by_index(turn >> 5, here)
+        spill = by_index(turn >> 5, here[3:] + here[:3])
+        right = pltpu.roll(jnp.where((turn & 31) == 0, spill, left), 127, 1)
         value = (1.0 - b) * left + b * right
         zs = z * 2 + slot
-        ready[q, zs] = value.astype(BF16)
-        kept[q, zs] = value if zs == 0 else pltpu.roll(value, 32 * zs, 1)
+        ready[q, zs] = pltpu.roll(value, (128 - low) & 127, 1).astype(BF16)
+        kept[q, zs] = pltpu.roll(value, (32 * zs + 128 - low) & 127, 1)
 
     sub = iota((8, 128), 0)
     which = jnp.where(sub < 4, group, (group + 1) & 3)
@@ -275,7 +291,6 @@
 ):
     me, deep = lax.axis_index("xy"), lax.axis_index("gz")
     bottom, last = lax.axis_size("xy") - 1, lax.axis_size("gz") - 1
-    lane = iota((IMG_ROWS, W), 1)
     for number, (ref, z) in enumerate(
         [(before, 0), (before, 1), (own, 0), (own, 1), (after, 0), (after, 1)]
     ):
@@ -284,15 +299,19 @@
             plane = jnp.where(deep == 0, 0.0, plane)
         if number >= 4:
             plane = jnp.where(deep == last, 0.0, plane)
-        shifted[number, 0] = jnp.where(lane == 0, 0.0, pltpu.roll(plane, 1, 1))
+        shifted[number, 0] = step_right(plane)
         shifted[number, 1] = plane
-        shifted[number, 2] = jnp.where(lane == W - 1, 0.0, pltpu.roll(plane, W - 1, 1))
+        shifted[number, 2] = step_left(plane)
     gain = jnp.concatenate([gain_in[...]] * 4, axis=1)
     lift = jnp.concatenate([lift_in[...]] * 4, axis=1)
     height = HID_ROWS * 8
 
-    @pl.loop(0, 4, unroll=UNROLL_ONE)
-    def _(p):
+    for p in range(4):
+        weight, bias = one[...], gain
+        if p == 0:
+            weight, bias = jnp.where(deep > 0, weight, 0), jnp.where(deep > 0, gain, 0.0)
+        if p == 3:
+            weight, bias = jnp.where(deep < last, weight, 0), jnp.where(deep < last, gain, 0.0)
         for b in range(3):
             start = HID_ROWS * b + 2
             stack = jnp.concatenate(
@@ -303,20 +322,16 @@
                 ],
                 axis=0,
             ).astype(BF16)
-            total = jnp.dot(one[...], stack, preferred_element_type=F32)
-            total = jnp.maximum(total.reshape(HID_ROWS, 8, W) + gain, 0.0)
-            keep = jnp.logical_and(
-                jnp.logical_or(p > 0, deep > 0), jnp.logical_or(p < 3, deep < last)
-            )
+            total = jnp.dot(weight, stack, preferred_element_type=F32)
+            total = jnp.maximum(total.reshape(HID_ROWS, 8, W) + bias, 0.0)
             layers = [total[r] for r in range(HID_ROWS)]
             if b == 0:
                 layers[0] = jnp.where(me > 0, layers[0], 0.0)
             if b == 2:
                 layers[-1] = jnp.where(me < bottom, layers[-1], 0.0)
-            total = jnp.where(keep, jnp.concatenate(layers, axis=0), 0.0)
+            total = jnp.concatenate(layers, axis=0)
             hidden[p, height * b : height * b + height, :] = total.astype(BF16)
 
-    edge = iota((64, W), 1)
 
     def sending(z, pair):
         rows = pl.ds(pl.multiple_of(16 * pair, 16), 16)
@@ -333,8 +348,7 @@
             rows = pl.ds(pl.multiple_of(128 * pair + 64 * b, 64), 80)
             stack = jnp.concatenate([hidden[z + d, rows, :] for d in range(3)], axis=0)
             total = jnp.dot(two[...], stack, preferred_element_type=F32)
-            left = jnp.where(edge == 0, 0.0, pltpu.roll(total[0:64], 1, 1))
-            right = jnp.where(edge == W - 1, 0.0, pltpu.roll(total[128:192], W - 1, 1))
+            left, right = step_right(total[0:64]), step_left(total[128:192])
             halves.append(total[64:128] + left + right + lift)
         rows = pl.ds(pl.multiple_of(16 * pair, 16), 16)
         for o in range(8):
@@ -455,6 +469,7 @@
         out_shape=pltpu.VMEM((sections, IMG_ROWS, W), BF16),
         in_specs=[smem(), vmem()],
         out_specs=vmem(),
+        compiler_params=pltpu.CompilerParams(vmem_limit_bytes=32 << 20),
         name="assemble",
     )(in_smem(places), in_vmem(received))
 

time: 42.6 us -> 42.3 us (level)
  waiting for transfers between devices: 13.6 us -> 14.2 us
  local copies, waits for them, and re-layouts: 3.44 us -> 2.88 us
    all_to_all x1, waiting for transfers between devices: 7.85 us -> 8.42 us  [on_device(): lax.all_to_all(outgoing, 'xy', split_axis=0, concat_axis=0, tiled=True)]
    add x1, local copies, waits for them, and re-layouts: 0.65 us -> 0.08 us  [on_device(): places = (holder * 2 + second.astype(jnp.int32)).reshape(-1)]
  transfers between devices with their start and end apart: 3 -> 3, of which waited for: 3 -> 3; matrix products, arithmetic and copies ran while one was open for 7% -> 6% of each run, Pallas kernels for 3% -> 4%
where the time goes in v6:
time: 42.3 us; the launch traced here: 41.8 us
  waiting for transfers between devices  14.2 us (34%)
  starting transfers between devices  13.8 us (33%)
  Pallas kernels  10.1 us (24%)
  local copies, waits for them, and re-layouts  2.88 us (7%)
  other arithmetic  0.76 us (2%)
    all_to_all x1, starting transfers between devices, on_device(): lax.all_to_all(outgoing, 'xy', split_axis=0, concat_axis=0, tiled=True)  12.6 us
    all_to_all x1, waiting for transfers between devices, on_device(): lax.all_to_all(outgoing, 'xy', split_axis=0, concat_axis=0, tiled=True)  8.42 us
    pallas_call x1, Pallas kernels, on_device(): pl.pallas_call(render_kernel, out_shape=jax.ShapeDtypeStruct((parts, 5, 8...  4.61 us
    pallas_call x1, Pallas kernels, on_device(): pl.pallas_call(conv_kernel, out_shape=jax.ShapeDtypeStruct((8, sections,...  3.15 us
    ppermute x1, waiting for transfers between devices, on_device(): lax.ppermute(image, 'gz', [(i, (i + 1) % depth) for i in range(depth)])  3.1 us
    ppermute x1, waiting for transfers between devices, on_device(): lax.ppermute(image, 'gz', [((i + 1) % depth, i) for i in range(depth)])  2.67 us
    pallas_call x1, Pallas kernels, on_device(): pl.pallas_call(band_kernel, out_shape=(pltpu.VMEM((HID_ROWS * 8, 9 * WIN_...  1.47 us
    unnamed x9, local copies, waits for them, and re-layouts  1.3 us
  transfers between devices with their start and end apart: 3, of which 3 were waited for; matrix products, arithmetic and copies ran while one was open for 6% of the time, Pallas kernels for 4%

profile of v6, /device:TPU:64, one launch (start us, length us, event | category | flops | bytes accessed | tf_op | source)
XLA Modules:
  0.0 41.8 jit_solution(1367890716368057298)
XLA Ops:
  0.0 4.6 %render.1 = bf16[32,5,8,128]{3,2,1,0:T(8,128)(2,1)} custom-call(s32[32]{0:T(128)} %owner_in.1, s32[2,1,1024]{2,1,0:T(1,128)} %bitcast.7, s32[2,1024]{1,0:T(2,128)} %tops_in.1, s32[2,1024]{1,0:T(2,128)} %lefts_in.1, s32[2,1024]{1,0:T(2,128)} %codes_in.1, bf16[2,512,512]{2,1,0:T(8,128)(2,1)} %bitcast.6), custom_call_target="tpu_custom_call" | custom-call | tf_op jit(solution)/shard_map/render/pallas_call | solution.py:401
  4.6 12.6 %all-to-all-start = ((bf16[32,5,8,128]{3,2,1,0:T(8,128)(2,1)}), bf16[32,5,8,128]{3,2,1,0:T(8,128)(2,1)S(1)}, u32[]{:S(2)}, u32[]{:S(2)}) async-start(bf16[32,5,8,128]{3,2,1,0:T(8,128)(2,1)} %render.1), calls=%async_computation | async-start | bytes 655360 | tf_op jit(solution)/shard_map/all_to_all | solution.py:433
  17.2 0.0 copy-start.2
  17.3 0.1 iota_compare_fusion.2
  17.3 0.6 %copy-done.2 = bf16[8,1,3,3,3]{0,4,3,2,1:T(4,128)(2,1)S(1)} copy-done((bf16[8,1,3,3,3]{0,4,3,2,1:T(4,128)(2,1)S(1)}, bf16[8,1,3,3,3]{0,4,3,2,1:T(4,128)(2,1)}, u32[]{:S(2)}) %copy-start.2) | copy-done | bytes 456
  18.0 0.0 copy-start.1
  18.0 0.7 %copy.17.flat_one = bf16[8,27]{1,0:T(8,128)(2,1)} copy(bf16[8,27]{0,1:T(8,128)(2,1)S(1)} %reshape.68) | data formatting | bytes 864 | tf_op jit(solution)/shard_map/reshape | solution.py:462
  18.6 0.0 copy-done.1
  18.7 0.0 copy-start
  18.7 0.1 broadcast_in_dim.38
  18.8 0.0 copy-start.3
  18.8 0.1 select_reduce_fusion.1
  18.9 0.6 %copy-done.3 = s32[32]{0:T(128)S(1)} copy-done((s32[32]{0:T(128)S(1)}, s32[32]{0:T(128)}, u32[]{:S(2)}) %copy-start.3) | copy-done | bytes 152
  19.4 0.3 select_reduce_fusion
  19.7 0.3 and_reduce_fusion
  20.0 0.1 add.28.table
  20.1 0.0 copy-done
  20.1 0.1 copy.16
  20.3 0.7 %copy.18.flat_two = bf16[8,216]{1,0:T(8,128)(2,1)} copy(bf16[8,216]{0,1:T(8,128)(2,1)S(1)} %reshape.69) | data formatting | bytes 6912 | tf_op jit(solution)/shard_map/reshape | solution.py:462
  20.9 1.5 %bands.1 = (bf16[176,216]{1,0:T(8,128)(2,1)S(1)}, bf16[192,240]{1,0:T(8,128)(2,1)S(1)}, f32[8,128]{1,0:T(8,128)S(1)}, f32[64,128]{1,0:T(8,128)S(1)}) custom-call(f32[8]{0:T(128)} %bias_one.1, f32[8]{0:T(128)} %bias_two.1, bf16[8,27]{1,0:T(8,128)(2,1)} %copy.17.flat_one, bf16[8,216]{1,0:T(8,128)(2,1)} %copy.18.flat_two), custom_call_target="tpu_custom_call" | custom-call | tf_op jit(solution)/shard_map/bands/pallas_call | solution.py:451
  22.4 8.4 %all-to-all-done.pool = bf16[32,5,8,128]{3,2,1,0:T(8,128)(2,1)S(1)} async-done(((bf16[32,5,8,128]{3,2,1,0:T(8,128)(2,1)}), bf16[32,5,8,128]{3,2,1,0:T(8,128)(2,1)S(1)}, u32[]{:S(2)}, u32[]{:S(2)}) %all-to-all-start) | async-done | bytes 327712 | tf_op jit(solution)/shard_map/all_to_all | solution.py:433
  30.8 0.9 %assemble.1.own = bf16[2,72,512]{2,1,0:T(8,128)(2,1)S(1)} custom-call(s32[192]{0:T(256)S(1)} %add.28.table, bf16[32,5,8,128]{3,2,1,0:T(8,128)(2,1)S(1)} %all-to-all-done.pool), custom_call_target="tpu_custom_call" | custom-call | tf_op jit(solution)/shard_map/assemble/pallas_call | solution.py:467
  31.7 1.2 %collective-permute-start.1 = (bf16[2,72,512]{2,1,0:T(8,128)(2,1)S(1)}, bf16[2,72,512]{2,1,0:T(8,128)(2,1)S(1)}, u32[]{:S(2)}, u32[]{:S(2)}) collective-permute-start(bf16[2,72,512]{2,1,0:T(8,128)(2,1)S(1)} %assemble.1.own), channel_id=1, source_target_pairs={{1,0},{2,1},{3,2},{4,3},{5,4},{6,5},{7,6},{8,7},{9,8},{10,9},{11,1... | collective-permute-start | bytes 442376 | tf_op jit(solution)/shard_map/ppermute | solution.py:477
  32.9 0.0 collective-permute-start
  32.9 2.7 %collective-permute-done.1.after = bf16[2,72,512]{2,1,0:T(8,128)(2,1)S(1)} collective-permute-done((bf16[2,72,512]{2,1,0:T(8,128)(2,1)S(1)}, bf16[2,72,512]{2,1,0:T(8,128)(2,1)S(1)}, u32[]{:S(2)}, u32[]{:S(2)}) %collective-permute-start.1) | collective-permute-done | bytes 147488 | tf_op jit(solution)/shard_map/ppermute | solution.py:477
  35.6 3.1 %collective-permute-done.before = bf16[2,72,512]{2,1,0:T(8,128)(2,1)S(1)} collective-permute-done((bf16[2,72,512]{2,1,0:T(8,128)(2,1)S(1)}, bf16[2,72,512]{2,1,0:T(8,128)(2,1)S(1)}, u32[]{:S(2)}, u32[]{:S(2)}) %collective-permute-start) | collective-permute-done | bytes 147488 | tf_op jit(solution)/shard_map/ppermute | solution.py:476
  38.7 3.1 %convolve.1 = bf16[8,2,64,512]{3,2,1,0:T(8,128)(2,1)} custom-call(f32[8,128]{1,0:T(8,128)S(1)} %get-tuple-element.19.gain_in, f32[64,128]{1,0:T(8,128)S(1)} %get-tuple-element.20.lift_in, bf16[2,72,512]{2,1,0:T(8,128)(2,1)S(1)} %collective-permute-done.before, bf16[2,72,512]{2,1,0:T(8,128)(2,1)S(1)} %assemble.1.own, ...), custom_call_target="tpu_custom_call" | custom-call | tf_op jit(solution)/shard_map/convolve/pallas_call | solution.py:479
  (6 shorter events, 0.1 us)
Async XLA Ops:
  4.6 26.2 %all-to-all-start = ((bf16[32,5,8,128]{3,2,1,0:T(8,128)(2,1)}), bf16[32,5,8,128]{3,2,1,0:T(8,128)(2,1)S(1)}, u32[]{:S(2)}, u32[]{:S(2)}) async-start(bf16[32,5,8,128]{3,2,1,0:T(8,128)(2,1)} %render.1), calls=%async_computation | async-start | bytes 655360 | tf_op jit(solution)/shard_map/all_to_all | solution.py:433
  17.2 0.7 %copy-start.2 = (bf16[8,1,3,3,3]{0,4,3,2,1:T(4,128)(2,1)S(1)}, bf16[8,1,3,3,3]{0,4,3,2,1:T(4,128)(2,1)}, u32[]{:S(2)}) copy-start(bf16[8,1,3,3,3]{0,4,3,2,1:T(4,128)(2,1)} %param.16) | copy-start | bytes 1300
  18.0 0.7 %copy-start.1 = (s32[2,1024,1]{1,2,0:T(1,128)S(1)}, s32[2,1024,1]{1,2,0:T(1,128)}, u32[]{:S(2)}) copy-start(s32[2,1024,1]{1,2,0:T(1,128)} %param.11) | copy-start | bytes 24580
  18.7 1.4 %copy-start = (bf16[8,8,3,3,3]{1,0,4,3,2:T(8,128)(2,1)S(1)}, bf16[8,8,3,3,3]{1,0,4,3,2:T(8,128)(2,1)}, u32[]{:S(2)}) copy-start(bf16[8,8,3,3,3]{1,0,4,3,2:T(8,128)(2,1)} %param.18) | copy-start | bytes 10372
  18.8 0.7 %copy-start.3 = (s32[32]{0:T(128)S(1)}, s32[32]{0:T(128)}, u32[]{:S(2)}) copy-start(s32[32]{0:T(128)} %owner_in.1) | copy-start | bytes 388
  31.7 3.8 %collective-permute-start.1 = (bf16[2,72,512]{2,1,0:T(8,128)(2,1)S(1)}, bf16[2,72,512]{2,1,0:T(8,128)(2,1)S(1)}, u32[]{:S(2)}, u32[]{:S(2)}) collective-permute-start(bf16[2,72,512]{2,1,0:T(8,128)(2,1)S(1)} %assemble.1.own), channel_id=1, source_target_pairs={{1,0},{2,1},{3,2},{4,3},{5,4},{6,5},{7,6},{8,7},{9,8},{10,9},{11,1... | collective-permute-start | bytes 442376 | tf_op jit(solution)/shard_map/ppermute | solution.py:477
  32.9 5.8 %collective-permute-start = (bf16[2,72,512]{2,1,0:T(8,128)(2,1)S(1)}, bf16[2,72,512]{2,1,0:T(8,128)(2,1)S(1)}, u32[]{:S(2)}, u32[]{:S(2)}) collective-permute-start(bf16[2,72,512]{2,1,0:T(8,128)(2,1)S(1)} %assemble.1.own), channel_id=1, source_target_pairs={{0,1},{1,2},{2,3},{3,4},{4,5},{5,6},{6,7},{7,8},{8,9},{9,10},{10,1... | collective-permute-start | bytes 442376 | tf_op jit(solution)/shard_map/ppermute | solution.py:476

commit v7 on v6

--- a/solution.py
+++ b/solution.py
@@ -13,7 +13,6 @@
 BATCH = 8
 MAIN_UNROLL = 8
 HALO_UNROLL = 4
-UNROLL_TWO = 8
 F32 = jnp.float32
 BF16 = jnp.bfloat16
 
@@ -306,59 +305,56 @@
     lift = jnp.concatenate([lift_in[...]] * 4, axis=1)
     height = HID_ROWS * 8
 
-    for p in range(4):
-        weight, bias = one[...], gain
-        if p == 0:
-            weight, bias = jnp.where(deep > 0, weight, 0), jnp.where(deep > 0, gain, 0.0)
-        if p == 3:
-            weight, bias = jnp.where(deep < last, weight, 0), jnp.where(deep < last, gain, 0.0)
-        for b in range(3):
-            start = HID_ROWS * b + 2
+    weights, biases = [one[...]] * 4, [gain] * 4
+    weights[0], biases[0] = jnp.where(deep > 0, one[...], 0), jnp.where(deep > 0, gain, 0.0)
+    weights[3], biases[3] = jnp.where(deep < last, one[...], 0), jnp.where(deep < last, gain, 0.0)
+
+    def first_layer(p, b):
+        start = HID_ROWS * b + 2
+        stack = jnp.concatenate(
+            [
+                shifted[p + d, f, start : start + WIN_ROWS, :]
+                for f in range(3)
+                for d in range(3)
+            ],
+            axis=0,
+        ).astype(BF16)
+        total = jnp.dot(weights[p], stack, preferred_element_type=F32)
+        total = jnp.maximum(total.reshape(HID_ROWS, 8, W) + biases[p], 0.0)
+        layers = [total[r] for r in range(HID_ROWS)]
+        if b == 0:
+            layers[0] = jnp.where(me > 0, layers[0], 0.0)
+        if b == 2:
+            layers[-1] = jnp.where(me < bottom, layers[-1], 0.0)
+        total = jnp.concatenate(layers, axis=0)
+        hidden[p, height * b : height * b + height, :] = total.astype(BF16)
+
+    def second_layer(z, pair):
+        halves = []
+        for b in (2 * pair, 2 * pair + 1):
             stack = jnp.concatenate(
-                [
-                    shifted[p + d, f, start : start + WIN_ROWS, :]
-                    for f in range(3)
-                    for d in range(3)
-                ],
-                axis=0,
-            ).astype(BF16)
-            total = jnp.dot(weight, stack, preferred_element_type=F32)
-            total = jnp.maximum(total.reshape(HID_ROWS, 8, W) + bias, 0.0)
-            layers = [total[r] for r in range(HID_ROWS)]
-            if b == 0:
-                layers[0] = jnp.where(me > 0, layers[0], 0.0)
-            if b == 2:
-                layers[-1] = jnp.where(me < bottom, layers[-1], 0.0)
-            total = jnp.concatenate(layers, axis=0)
-            hidden[p, height * b : height * b + height, :] = total.astype(BF16)
-
-
-    def sending(z, pair):
-        rows = pl.ds(pl.multiple_of(16 * pair, 16), 16)
-        return pltpu.make_async_copy(
-            stage.at[:, z, rows, :], out.at[:, z, rows, :], sent.at[4 * z + pair]
-        )
-
-    @pl.loop(0, 8, unroll=UNROLL_TWO)
-    def _(turn):
-        z = turn >> 2
-        pair = turn & 3
-        halves = []
-        for b in range(2):
-            rows = pl.ds(pl.multiple_of(128 * pair + 64 * b, 64), 80)
-            stack = jnp.concatenate([hidden[z + d, rows, :] for d in range(3)], axis=0)
+                [hidden[z + d, 64 * b : 64 * b + 80, :] for d in range(3)], axis=0
+            )
             total = jnp.dot(two[...], stack, preferred_element_type=F32)
             left, right = step_right(total[0:64]), step_left(total[128:192])
             halves.append(total[64:128] + left + right + lift)
-        rows = pl.ds(pl.multiple_of(16 * pair, 16), 16)
+        rows = pl.ds(16 * pair, 16)
         for o in range(8):
             both = jnp.concatenate([half[8 * o : 8 * o + 8] for half in halves], axis=0)
             stage[o, z, rows, :] = both.astype(BF16)
-        sending(z, pair).start()
-
-    @pl.loop(0, 8)
-    def _(turn):
-        sending(turn >> 2, turn & 3).wait()
+        copy = pltpu.make_async_copy(
+            stage.at[:, z, rows, :], out.at[:, z, rows, :], sent.at[4 * z + pair]
+        )
+        copy.start()
+        return copy
+
+    copies = []
+    for b, pairs in enumerate(((0,), (1,), (2, 3))):
+        for p in range(4):
+            first_layer(p, b)
+        copies += [second_layer(z, pair) for pair in pairs for z in range(2)]
+    for copy in copies:
+        copy.wait()
 
 
 def smem():

time: 42.3 us -> 42.1 us (level)
  no operation moved by 1% of the time
where the time goes in v7:
time: 42.1 us; the launch traced here: 41.7 us
  waiting for transfers between devices  14.2 us (34%)
  starting transfers between devices  13.8 us (33%)
  Pallas kernels  10 us (24%)
  local copies, waits for them, and re-layouts  2.88 us (7%)
  other arithmetic  0.76 us (2%)
    all_to_all x1, starting transfers between devices, on_device(): lax.all_to_all(outgoing, 'xy', split_axis=0, concat_axis=0, tiled=True)  12.6 us
    all_to_all x1, waiting for transfers between devices, on_device(): lax.all_to_all(outgoing, 'xy', split_axis=0, concat_axis=0, tiled=True)  8.41 us
    pallas_call x1, Pallas kernels, on_device(): pl.pallas_call(render_kernel, out_shape=jax.ShapeDtypeStruct((parts, 5, 8...  4.6 us
    ppermute x1, waiting for transfers between devices, on_device(): lax.ppermute(image, 'gz', [(i, (i + 1) % depth) for i in range(depth)])  3.1 us
    pallas_call x1, Pallas kernels, on_device(): pl.pallas_call(conv_kernel, out_shape=jax.ShapeDtypeStruct((8, sections,...  3.03 us
    ppermute x1, waiting for transfers between devices, on_device(): lax.ppermute(image, 'gz', [((i + 1) % depth, i) for i in range(depth)])  2.67 us
    pallas_call x1, Pallas kernels, on_device(): pl.pallas_call(band_kernel, out_shape=(pltpu.VMEM((HID_ROWS * 8, 9 * WIN_...  1.47 us
    unnamed x9, local copies, waits for them, and re-layouts  1.3 us
  transfers between devices with their start and end apart: 3, of which 3 were waited for; matrix products, arithmetic and copies ran while one was open for 6% of the time, Pallas kernels for 4%

profile of v7, /device:TPU:64, one launch (start us, length us, event | category | flops | bytes accessed | tf_op | source)
XLA Modules:
  0.0 41.7 jit_solution(6525744886177322148)
XLA Ops:
  0.0 4.6 %render.1 = bf16[32,5,8,128]{3,2,1,0:T(8,128)(2,1)} custom-call(s32[32]{0:T(128)} %owner_in.1, s32[2,1,1024]{2,1,0:T(1,128)} %bitcast.7, s32[2,1024]{1,0:T(2,128)} %tops_in.1, s32[2,1024]{1,0:T(2,128)} %lefts_in.1, s32[2,1024]{1,0:T(2,128)} %codes_in.1, bf16[2,512,512]{2,1,0:T(8,128)(2,1)} %bitcast.6), custom_call_target="tpu_custom_call" | custom-call | tf_op jit(solution)/shard_map/render/pallas_call | solution.py:397
  4.6 12.6 %all-to-all-start = ((bf16[32,5,8,128]{3,2,1,0:T(8,128)(2,1)}), bf16[32,5,8,128]{3,2,1,0:T(8,128)(2,1)S(1)}, u32[]{:S(2)}, u32[]{:S(2)}) async-start(bf16[32,5,8,128]{3,2,1,0:T(8,128)(2,1)} %render.1), calls=%async_computation | async-start | bytes 655360 | tf_op jit(solution)/shard_map/all_to_all | solution.py:429
  17.2 0.0 copy-start.2
  17.3 0.1 iota_compare_fusion.2
  17.3 0.6 %copy-done.2 = bf16[8,1,3,3,3]{0,4,3,2,1:T(4,128)(2,1)S(1)} copy-done((bf16[8,1,3,3,3]{0,4,3,2,1:T(4,128)(2,1)S(1)}, bf16[8,1,3,3,3]{0,4,3,2,1:T(4,128)(2,1)}, u32[]{:S(2)}) %copy-start.2) | copy-done | bytes 456
  17.9 0.0 copy-start.1
  18.0 0.7 %copy.17.flat_one = bf16[8,27]{1,0:T(8,128)(2,1)} copy(bf16[8,27]{0,1:T(8,128)(2,1)S(1)} %reshape.68) | data formatting | bytes 864 | tf_op jit(solution)/shard_map/reshape | solution.py:458
  18.6 0.0 copy-done.1
  18.7 0.0 copy-start
  18.7 0.1 broadcast_in_dim.38
  18.8 0.0 copy-start.3
  18.8 0.1 select_reduce_fusion.1
  18.9 0.6 %copy-done.3 = s32[32]{0:T(128)S(1)} copy-done((s32[32]{0:T(128)S(1)}, s32[32]{0:T(128)}, u32[]{:S(2)}) %copy-start.3) | copy-done | bytes 152
  19.4 0.3 select_reduce_fusion
  19.7 0.3 and_reduce_fusion
  20.0 0.1 add.28.table
  20.1 0.0 copy-done
  20.1 0.1 copy.16
  20.3 0.7 %copy.18.flat_two = bf16[8,216]{1,0:T(8,128)(2,1)} copy(bf16[8,216]{0,1:T(8,128)(2,1)S(1)} %reshape.69) | data formatting | bytes 6912 | tf_op jit(solution)/shard_map/reshape | solution.py:458
  20.9 1.5 %bands.1 = (bf16[176,216]{1,0:T(8,128)(2,1)S(1)}, bf16[192,240]{1,0:T(8,128)(2,1)S(1)}, f32[8,128]{1,0:T(8,128)S(1)}, f32[64,128]{1,0:T(8,128)S(1)}) custom-call(f32[8]{0:T(128)} %bias_one.1, f32[8]{0:T(128)} %bias_two.1, bf16[8,27]{1,0:T(8,128)(2,1)} %copy.17.flat_one, bf16[8,216]{1,0:T(8,128)(2,1)} %copy.18.flat_two), custom_call_target="tpu_custom_call" | custom-call | tf_op jit(solution)/shard_map/bands/pallas_call | solution.py:447
  22.4 8.4 %all-to-all-done.pool = bf16[32,5,8,128]{3,2,1,0:T(8,128)(2,1)S(1)} async-done(((bf16[32,5,8,128]{3,2,1,0:T(8,128)(2,1)}), bf16[32,5,8,128]{3,2,1,0:T(8,128)(2,1)S(1)}, u32[]{:S(2)}, u32[]{:S(2)}) %all-to-all-start) | async-done | bytes 327712 | tf_op jit(solution)/shard_map/all_to_all | solution.py:429
  30.8 0.9 %assemble.1.own = bf16[2,72,512]{2,1,0:T(8,128)(2,1)S(1)} custom-call(s32[192]{0:T(256)S(1)} %add.28.table, bf16[32,5,8,128]{3,2,1,0:T(8,128)(2,1)S(1)} %all-to-all-done.pool), custom_call_target="tpu_custom_call" | custom-call | tf_op jit(solution)/shard_map/assemble/pallas_call | solution.py:463
  31.7 1.2 %collective-permute-start.1 = (bf16[2,72,512]{2,1,0:T(8,128)(2,1)S(1)}, bf16[2,72,512]{2,1,0:T(8,128)(2,1)S(1)}, u32[]{:S(2)}, u32[]{:S(2)}) collective-permute-start(bf16[2,72,512]{2,1,0:T(8,128)(2,1)S(1)} %assemble.1.own), channel_id=1, source_target_pairs={{1,0},{2,1},{3,2},{4,3},{5,4},{6,5},{7,6},{8,7},{9,8},{10,9},{11,1... | collective-permute-start | bytes 442376 | tf_op jit(solution)/shard_map/ppermute | solution.py:473
  32.9 0.0 collective-permute-start
  32.9 2.7 %collective-permute-done.1.after = bf16[2,72,512]{2,1,0:T(8,128)(2,1)S(1)} collective-permute-done((bf16[2,72,512]{2,1,0:T(8,128)(2,1)S(1)}, bf16[2,72,512]{2,1,0:T(8,128)(2,1)S(1)}, u32[]{:S(2)}, u32[]{:S(2)}) %collective-permute-start.1) | collective-permute-done | bytes 147488 | tf_op jit(solution)/shard_map/ppermute | solution.py:473
  35.6 3.1 %collective-permute-done.before = bf16[2,72,512]{2,1,0:T(8,128)(2,1)S(1)} collective-permute-done((bf16[2,72,512]{2,1,0:T(8,128)(2,1)S(1)}, bf16[2,72,512]{2,1,0:T(8,128)(2,1)S(1)}, u32[]{:S(2)}, u32[]{:S(2)}) %collective-permute-start) | collective-permute-done | bytes 147488 | tf_op jit(solution)/shard_map/ppermute | solution.py:472
  38.7 3.0 %convolve.1 = bf16[8,2,64,512]{3,2,1,0:T(8,128)(2,1)} custom-call(f32[8,128]{1,0:T(8,128)S(1)} %get-tuple-element.19.gain_in, f32[64,128]{1,0:T(8,128)S(1)} %get-tuple-element.20.lift_in, bf16[2,72,512]{2,1,0:T(8,128)(2,1)S(1)} %collective-permute-done.before, bf16[2,72,512]{2,1,0:T(8,128)(2,1)S(1)} %assemble.1.own, ...), custom_call_target="tpu_custom_call" | custom-call | tf_op jit(solution)/shard_map/convolve/pallas_call | solution.py:475
  (6 shorter events, 0.1 us)
Async XLA Ops:
  4.6 26.2 %all-to-all-start = ((bf16[32,5,8,128]{3,2,1,0:T(8,128)(2,1)}), bf16[32,5,8,128]{3,2,1,0:T(8,128)(2,1)S(1)}, u32[]{:S(2)}, u32[]{:S(2)}) async-start(bf16[32,5,8,128]{3,2,1,0:T(8,128)(2,1)} %render.1), calls=%async_computation | async-start | bytes 655360 | tf_op jit(solution)/shard_map/all_to_all | solution.py:429
  17.2 0.7 %copy-start.2 = (bf16[8,1,3,3,3]{0,4,3,2,1:T(4,128)(2,1)S(1)}, bf16[8,1,3,3,3]{0,4,3,2,1:T(4,128)(2,1)}, u32[]{:S(2)}) copy-start(bf16[8,1,3,3,3]{0,4,3,2,1:T(4,128)(2,1)} %param.16) | copy-start | bytes 1300
  17.9 0.7 %copy-start.1 = (s32[2,1024,1]{1,2,0:T(1,128)S(1)}, s32[2,1024,1]{1,2,0:T(1,128)}, u32[]{:S(2)}) copy-start(s32[2,1024,1]{1,2,0:T(1,128)} %param.11) | copy-start | bytes 24580
  18.7 1.4 %copy-start = (bf16[8,8,3,3,3]{1,0,4,3,2:T(8,128)(2,1)S(1)}, bf16[8,8,3,3,3]{1,0,4,3,2:T(8,128)(2,1)}, u32[]{:S(2)}) copy-start(bf16[8,8,3,3,3]{1,0,4,3,2:T(8,128)(2,1)} %param.18) | copy-start | bytes 10372
  18.8 0.7 %copy-start.3 = (s32[32]{0:T(128)S(1)}, s32[32]{0:T(128)}, u32[]{:S(2)}) copy-start(s32[32]{0:T(128)} %owner_in.1) | copy-start | bytes 388
  31.7 3.9 %collective-permute-start.1 = (bf16[2,72,512]{2,1,0:T(8,128)(2,1)S(1)}, bf16[2,72,512]{2,1,0:T(8,128)(2,1)S(1)}, u32[]{:S(2)}, u32[]{:S(2)}) collective-permute-start(bf16[2,72,512]{2,1,0:T(8,128)(2,1)S(1)} %assemble.1.own), channel_id=1, source_target_pairs={{1,0},{2,1},{3,2},{4,3},{5,4},{6,5},{7,6},{8,7},{9,8},{10,9},{11,1... | collective-permute-start | bytes 442376 | tf_op jit(solution)/shard_map/ppermute | solution.py:473
  32.9 5.8 %collective-permute-start = (bf16[2,72,512]{2,1,0:T(8,128)(2,1)S(1)}, bf16[2,72,512]{2,1,0:T(8,128)(2,1)S(1)}, u32[]{:S(2)}, u32[]{:S(2)}) collective-permute-start(bf16[2,72,512]{2,1,0:T(8,128)(2,1)S(1)} %assemble.1.own), channel_id=1, source_target_pairs={{0,1},{1,2},{2,3},{3,4},{4,5},{5,6},{6,7},{7,8},{8,9},{9,10},{10,1... | collective-permute-start | bytes 442376 | tf_op jit(solution)/shard_map/ppermute | solution.py:472

commit v8 on v7

--- a/solution.py
+++ b/solution.py
@@ -127,7 +127,8 @@
         + (sums[24 * slot + 16 : 24 * slot + 24] << 16)
         for slot in range(2)
     ]
-    found[...] = jnp.where(iota((8, 128), 0) < 2, pair[0], pltpu.roll(pair[1], 2, 0))
+    merged = jnp.where(iota((8, 128), 0) < 2, pair[0], pltpu.roll(pair[1], 2, 0))
+    found[...] = merged[0:4]
     listing = pltpu.make_async_copy(found, table, listed.at[0])
     listing.start()
 
@@ -349,9 +350,12 @@
         return copy
 
     copies = []
+    for p in range(4):
+        first_layer(p, 0)
     for b, pairs in enumerate(((0,), (1,), (2, 3))):
-        for p in range(4):
-            first_layer(p, b)
+        if b < 2:
+            for p in range(4):
+                first_layer(p, b + 1)
         copies += [second_layer(z, pair) for pair in pairs for z in range(2)]
     for copy in copies:
         copy.wait()
@@ -409,8 +413,8 @@
             pltpu.VMEM((sections, 4, 512, 128), F32),
             pltpu.VMEM((parts, 2 * sections, 8, 128), F32),
             pltpu.VMEM((parts, 5, 8, 128), BF16),
-            pltpu.VMEM((8, 128), jnp.int32),
-            pltpu.SMEM((8, 128), jnp.int32),
+            pltpu.VMEM((2 * sections, 128), jnp.int32),
+            pltpu.SMEM((2 * sections, 128), jnp.int32),
             pltpu.SemaphoreType.DMA((5,)),
             pltpu.SemaphoreType.DMA((2 * sections,)),
             pltpu.SemaphoreType.DMA((1,)),

time: 42.1 us -> 42.2 us (level)
  no operation moved by 1% of the time
where the time goes in v8:
time: 42.2 us; the launch traced here: 41.7 us
  waiting for transfers between devices  14.2 us (34%)
  starting transfers between devices  13.8 us (33%)
  Pallas kernels  10 us (24%)
  local copies, waits for them, and re-layouts  2.88 us (7%)
  other arithmetic  0.76 us (2%)
    all_to_all x1, starting transfers between devices, on_device(): lax.all_to_all(outgoing, 'xy', split_axis=0, concat_axis=0, tiled=True)  12.6 us
    all_to_all x1, waiting for transfers between devices, on_device(): lax.all_to_all(outgoing, 'xy', split_axis=0, concat_axis=0, tiled=True)  8.43 us
    pallas_call x1, Pallas kernels, on_device(): pl.pallas_call(render_kernel, out_shape=jax.ShapeDtypeStruct((parts, 5, 8...  4.58 us
    ppermute x1, waiting for transfers between devices, on_device(): lax.ppermute(image, 'gz', [(i, (i + 1) % depth) for i in range(depth)])  3.1 us
    pallas_call x1, Pallas kernels, on_device(): pl.pallas_call(conv_kernel, out_shape=jax.ShapeDtypeStruct((8, sections,...  3.08 us
    ppermute x1, waiting for transfers between devices, on_device(): lax.ppermute(image, 'gz', [((i + 1) % depth, i) for i in range(depth)])  2.67 us
    pallas_call x1, Pallas kernels, on_device(): pl.pallas_call(band_kernel, out_shape=(pltpu.VMEM((HID_ROWS * 8, 9 * WIN_...  1.47 us
    unnamed x9, local copies, waits for them, and re-layouts  1.3 us
  transfers between devices with their start and end apart: 3, of which 3 were waited for; matrix products, arithmetic and copies ran while one was open for 6% of the time, Pallas kernels for 4%

profile of v8, /device:TPU:64, one launch (start us, length us, event | category | flops | bytes accessed | tf_op | source)
XLA Modules:
  0.0 41.7 jit_solution(14808855802943494025)
XLA Ops:
  0.0 4.6 %render.1 = bf16[32,5,8,128]{3,2,1,0:T(8,128)(2,1)} custom-call(s32[32]{0:T(128)} %owner_in.1, s32[2,1,1024]{2,1,0:T(1,128)} %bitcast.7, s32[2,1024]{1,0:T(2,128)} %tops_in.1, s32[2,1024]{1,0:T(2,128)} %lefts_in.1, s32[2,1024]{1,0:T(2,128)} %codes_in.1, bf16[2,512,512]{2,1,0:T(8,128)(2,1)} %bitcast.6), custom_call_target="tpu_custom_call" | custom-call | tf_op jit(solution)/shard_map/render/pallas_call | solution.py:401
  4.6 12.6 %all-to-all-start = ((bf16[32,5,8,128]{3,2,1,0:T(8,128)(2,1)}), bf16[32,5,8,128]{3,2,1,0:T(8,128)(2,1)S(1)}, u32[]{:S(2)}, u32[]{:S(2)}) async-start(bf16[32,5,8,128]{3,2,1,0:T(8,128)(2,1)} %render.1), calls=%async_computation | async-start | bytes 655360 | tf_op jit(solution)/shard_map/all_to_all | solution.py:433
  17.2 0.0 copy-start.2
  17.2 0.1 iota_compare_fusion.2
  17.3 0.6 %copy-done.2 = bf16[8,1,3,3,3]{0,4,3,2,1:T(4,128)(2,1)S(1)} copy-done((bf16[8,1,3,3,3]{0,4,3,2,1:T(4,128)(2,1)S(1)}, bf16[8,1,3,3,3]{0,4,3,2,1:T(4,128)(2,1)}, u32[]{:S(2)}) %copy-start.2) | copy-done | bytes 456
  17.9 0.0 copy-start.1
  17.9 0.7 %copy.17.flat_one = bf16[8,27]{1,0:T(8,128)(2,1)} copy(bf16[8,27]{0,1:T(8,128)(2,1)S(1)} %reshape.68) | data formatting | bytes 864 | tf_op jit(solution)/shard_map/reshape | solution.py:462
  18.6 0.0 copy-done.1
  18.6 0.0 copy-start
  18.6 0.1 broadcast_in_dim.38
  18.7 0.0 copy-start.3
  18.7 0.1 select_reduce_fusion.1
  18.8 0.6 %copy-done.3 = s32[32]{0:T(128)S(1)} copy-done((s32[32]{0:T(128)S(1)}, s32[32]{0:T(128)}, u32[]{:S(2)}) %copy-start.3) | copy-done | bytes 152
  19.4 0.3 select_reduce_fusion
  19.7 0.3 and_reduce_fusion
  19.9 0.1 add.28.table
  20.0 0.0 copy-done
  20.0 0.1 copy.16
  20.2 0.7 %copy.18.flat_two = bf16[8,216]{1,0:T(8,128)(2,1)} copy(bf16[8,216]{0,1:T(8,128)(2,1)S(1)} %reshape.69) | data formatting | bytes 6912 | tf_op jit(solution)/shard_map/reshape | solution.py:462
  20.9 1.5 %bands.1 = (bf16[176,216]{1,0:T(8,128)(2,1)S(1)}, bf16[192,240]{1,0:T(8,128)(2,1)S(1)}, f32[8,128]{1,0:T(8,128)S(1)}, f32[64,128]{1,0:T(8,128)S(1)}) custom-call(f32[8]{0:T(128)} %bias_one.1, f32[8]{0:T(128)} %bias_two.1, bf16[8,27]{1,0:T(8,128)(2,1)} %copy.17.flat_one, bf16[8,216]{1,0:T(8,128)(2,1)} %copy.18.flat_two), custom_call_target="tpu_custom_call" | custom-call | tf_op jit(solution)/shard_map/bands/pallas_call | solution.py:451
  22.4 8.4 %all-to-all-done.pool = bf16[32,5,8,128]{3,2,1,0:T(8,128)(2,1)S(1)} async-done(((bf16[32,5,8,128]{3,2,1,0:T(8,128)(2,1)}), bf16[32,5,8,128]{3,2,1,0:T(8,128)(2,1)S(1)}, u32[]{:S(2)}, u32[]{:S(2)}) %all-to-all-start) | async-done | bytes 327712 | tf_op jit(solution)/shard_map/all_to_all | solution.py:433
  30.8 0.9 %assemble.1.own = bf16[2,72,512]{2,1,0:T(8,128)(2,1)S(1)} custom-call(s32[192]{0:T(256)S(1)} %add.28.table, bf16[32,5,8,128]{3,2,1,0:T(8,128)(2,1)S(1)} %all-to-all-done.pool), custom_call_target="tpu_custom_call" | custom-call | tf_op jit(solution)/shard_map/assemble/pallas_call | solution.py:467
  31.7 1.2 %collective-permute-start.1 = (bf16[2,72,512]{2,1,0:T(8,128)(2,1)S(1)}, bf16[2,72,512]{2,1,0:T(8,128)(2,1)S(1)}, u32[]{:S(2)}, u32[]{:S(2)}) collective-permute-start(bf16[2,72,512]{2,1,0:T(8,128)(2,1)S(1)} %assemble.1.own), channel_id=1, source_target_pairs={{1,0},{2,1},{3,2},{4,3},{5,4},{6,5},{7,6},{8,7},{9,8},{10,9},{11,1... | collective-permute-start | bytes 442376 | tf_op jit(solution)/shard_map/ppermute | solution.py:477
  32.9 0.0 collective-permute-start
  32.9 2.7 %collective-permute-done.1.after = bf16[2,72,512]{2,1,0:T(8,128)(2,1)S(1)} collective-permute-done((bf16[2,72,512]{2,1,0:T(8,128)(2,1)S(1)}, bf16[2,72,512]{2,1,0:T(8,128)(2,1)S(1)}, u32[]{:S(2)}, u32[]{:S(2)}) %collective-permute-start.1) | collective-permute-done | bytes 147488 | tf_op jit(solution)/shard_map/ppermute | solution.py:477
  35.5 3.1 %collective-permute-done.before = bf16[2,72,512]{2,1,0:T(8,128)(2,1)S(1)} collective-permute-done((bf16[2,72,512]{2,1,0:T(8,128)(2,1)S(1)}, bf16[2,72,512]{2,1,0:T(8,128)(2,1)S(1)}, u32[]{:S(2)}, u32[]{:S(2)}) %collective-permute-start) | collective-permute-done | bytes 147488 | tf_op jit(solution)/shard_map/ppermute | solution.py:476
  38.6 3.1 %convolve.1 = bf16[8,2,64,512]{3,2,1,0:T(8,128)(2,1)} custom-call(f32[8,128]{1,0:T(8,128)S(1)} %get-tuple-element.19.gain_in, f32[64,128]{1,0:T(8,128)S(1)} %get-tuple-element.20.lift_in, bf16[2,72,512]{2,1,0:T(8,128)(2,1)S(1)} %collective-permute-done.before, bf16[2,72,512]{2,1,0:T(8,128)(2,1)S(1)} %assemble.1.own, ...), custom_call_target="tpu_custom_call" | custom-call | tf_op jit(solution)/shard_map/convolve/pallas_call | solution.py:479
  (6 shorter events, 0.1 us)
Async XLA Ops:
  4.6 26.2 %all-to-all-start = ((bf16[32,5,8,128]{3,2,1,0:T(8,128)(2,1)}), bf16[32,5,8,128]{3,2,1,0:T(8,128)(2,1)S(1)}, u32[]{:S(2)}, u32[]{:S(2)}) async-start(bf16[32,5,8,128]{3,2,1,0:T(8,128)(2,1)} %render.1), calls=%async_computation | async-start | bytes 655360 | tf_op jit(solution)/shard_map/all_to_all | solution.py:433
  17.2 0.7 %copy-start.2 = (bf16[8,1,3,3,3]{0,4,3,2,1:T(4,128)(2,1)S(1)}, bf16[8,1,3,3,3]{0,4,3,2,1:T(4,128)(2,1)}, u32[]{:S(2)}) copy-start(bf16[8,1,3,3,3]{0,4,3,2,1:T(4,128)(2,1)} %param.16) | copy-start | bytes 1300
  17.9 0.7 %copy-start.1 = (s32[2,1024,1]{1,2,0:T(1,128)S(1)}, s32[2,1024,1]{1,2,0:T(1,128)}, u32[]{:S(2)}) copy-start(s32[2,1024,1]{1,2,0:T(1,128)} %param.11) | copy-start | bytes 24580
  18.6 1.4 %copy-start = (bf16[8,8,3,3,3]{1,0,4,3,2:T(8,128)(2,1)S(1)}, bf16[8,8,3,3,3]{1,0,4,3,2:T(8,128)(2,1)}, u32[]{:S(2)}) copy-start(bf16[8,8,3,3,3]{1,0,4,3,2:T(8,128)(2,1)} %param.18) | copy-start | bytes 10372
  18.7 0.7 %copy-start.3 = (s32[32]{0:T(128)S(1)}, s32[32]{0:T(128)}, u32[]{:S(2)}) copy-start(s32[32]{0:T(128)} %owner_in.1) | copy-start | bytes 388
  31.7 3.8 %collective-permute-start.1 = (bf16[2,72,512]{2,1,0:T(8,128)(2,1)S(1)}, bf16[2,72,512]{2,1,0:T(8,128)(2,1)S(1)}, u32[]{:S(2)}, u32[]{:S(2)}) collective-permute-start(bf16[2,72,512]{2,1,0:T(8,128)(2,1)S(1)} %assemble.1.own), channel_id=1, source_target_pairs={{1,0},{2,1},{3,2},{4,3},{5,4},{6,5},{7,6},{8,7},{9,8},{10,9},{11,1... | collective-permute-start | bytes 442376 | tf_op jit(solution)/shard_map/ppermute | solution.py:477
  32.9 5.8 %collective-permute-start = (bf16[2,72,512]{2,1,0:T(8,128)(2,1)S(1)}, bf16[2,72,512]{2,1,0:T(8,128)(2,1)S(1)}, u32[]{:S(2)}, u32[]{:S(2)}) collective-permute-start(bf16[2,72,512]{2,1,0:T(8,128)(2,1)S(1)} %assemble.1.own), channel_id=1, source_target_pairs={{0,1},{1,2},{2,3},{3,4},{4,5},{5,6},{6,7},{7,8},{8,9},{9,10},{10,1... | collective-permute-start | bytes 442376 | tf_op jit(solution)/shard_map/ppermute | solution.py:476
